TPU v7x, 128 devices: a whole 4x4x4 slice. The times are simulated.
128 devices in a mesh: teacher: 4 (over y), dp: 32 (over x, z, core).
Axes of the slice: x: 4, y: 4, z: 4, core: 2. Of those that a mesh axis runs over, the one named last changes fastest.
Arguments:
- hid_whisper: bfloat16 [16384, 1280], P(('teacher', 'dp')), may hold values from -6 to 6
- hid_beats: bfloat16 [16384, 768], P(('teacher', 'dp')), may hold values from -6 to 6
- hid_wavlm: bfloat16 [16384, 1024], P(('teacher', 'dp')), may hold values from -6 to 6
- up_whisper: bfloat16 [1280, 5120], P(None, 'teacher'), may hold values from -0.15625 to 0.15625
- down_whisper: bfloat16 [5120, 1280], P('teacher'), may hold values from -0.078125 to 0.078125
- up_beats: bfloat16 [768, 3072], P(None, 'teacher'), may hold values from -0.21875 to 0.21875
- down_beats: bfloat16 [3072, 768], P('teacher'), may hold values from -0.109375 to 0.109375
- up_wavlm: bfloat16 [1024, 4096], P(None, 'teacher'), may hold values from -0.1875 to 0.1875
- down_wavlm: bfloat16 [4096, 1024], P('teacher'), may hold values from -0.09375 to 0.09375
- clip_len: int32 [128], P(('teacher', 'dp')), may hold values from 16 to 128
- send_counts: int32 [4, 32, 32], P('teacher'), may hold values from 0 to 8, as said below
- student_in: bfloat16 [16384, 512], P(('teacher', 'dp')), may hold values from -24 to 24
- w_in: bfloat16 [512, 1536], P('dp'), may hold values from -0.25 to 0.25
- w_out: bfloat16 [1536, 512], P('dp'), may hold values from -0.15625 to 0.15625
- w_head: bfloat16 [512, 3072], P('dp'), may hold values from -0.25 to 0.25
Outputs:
- grad_in: float32 [512, 1536], P('dp')
- grad_out: float32 [1536, 512], P('dp')
- grad_head: float32 [512, 3072], P('dp')
Inputs may be any that keep to these rules, and one draw needn't show every extreme that they name: In every group t, each source s hands 128 frames in all (the sum over o of send_counts[t,s,o]), each owner o receives 128 frames in all, and in every group some source hands exactly 8 frames to some owner.
All inputs are finite; a program needn't handle non-finite values.
Results may differ from a plain program's by a relative error of at most 0.0031.
Values may be sent and summed in bfloat16 or wider, within the bound.
A program may use at most 128 MiB of HBM per device.

v0:
```python
import jax
import jax.numpy as jnp
from jax import lax
from jax.sharding import PartitionSpec as P

WH = 1280
WB = 768
WL = 1024


EPS = 1e-05


def layer_norm(values):
    wide = values.astype(jnp.float32)
    center = wide - jnp.mean(wide, axis=-1, keepdims=True)
    spread = jnp.mean(center * center, axis=-1, keepdims=True)
    return center * lax.rsqrt(spread + EPS)


def swoosh_low(pre_act):
    return jax.nn.softplus(pre_act - 4.0) - 0.08 * pre_act - 0.035


def swoosh_slope(pre_act):
    return jax.nn.sigmoid(pre_act - 4.0) - 0.08


def column_scale():
    return jnp.concatenate(
        [
            jnp.full((WH,), 2.0 / WH, jnp.float32),
            jnp.full((WB,), 2.0 / WB, jnp.float32),
            jnp.full((WL,), 2.0 / WL, jnp.float32),
        ]
    )


def body(
    hid_whisper,
    hid_beats,
    hid_wavlm,
    up_whisper,
    down_whisper,
    up_beats,
    down_beats,
    up_wavlm,
    down_wavlm,
    clip_len,
    send_counts,
    student_in,
    w_in,
    w_out,
    w_head,
):
    owner_count = lax.axis_size("dp")
    owner_index = lax.axis_index("dp")
    frames = hid_whisper.shape[0]
    capacity = 2 * frames // owner_count
    normed_whisper = layer_norm(hid_whisper).astype(jnp.bfloat16)
    normed_beats = layer_norm(hid_beats).astype(jnp.bfloat16)
    normed_wavlm = layer_norm(hid_wavlm).astype(jnp.bfloat16)
    gathered = (
        lax.all_gather(normed_whisper, "teacher", axis=0, tiled=True),
        lax.all_gather(normed_beats, "teacher", axis=0, tiled=True),
        lax.all_gather(normed_wavlm, "teacher", axis=0, tiled=True),
    )
    pairs = ((up_whisper, down_whisper), (up_beats, down_beats), (up_wavlm, down_wavlm))
    pieces = []
    for rows_all, (up_proj, down_proj) in zip(gathered, pairs):
        hidden = jax.nn.gelu(
            jnp.dot(rows_all, up_proj, preferred_element_type=jnp.float32), approximate=False
        ).astype(jnp.bfloat16)
        pieces.append(jnp.dot(hidden, down_proj, preferred_element_type=jnp.float32))
    summed = lax.psum_scatter(
        jnp.concatenate(pieces, axis=1), "teacher", scatter_dimension=0, tiled=True
    )
    residual = jnp.concatenate([hid_whisper, hid_beats, hid_wavlm], axis=1).astype(jnp.float32)
    targets = (summed + residual).astype(jnp.bfloat16)
    positions = jnp.arange(frames, dtype=jnp.int32)
    clip_slots = frames // clip_len.shape[0]
    lengths = jnp.repeat(clip_len, clip_slots, total_repeat_length=frames)
    valid = positions % clip_slots < lengths
    table = send_counts[0]
    send_row = lax.dynamic_index_in_dim(table, owner_index, 0, keepdims=False)
    recv_col = lax.dynamic_index_in_dim(table, owner_index, 1, keepdims=False)
    slots = jnp.arange(capacity, dtype=jnp.int32)
    send_start = jnp.cumsum(send_row, dtype=jnp.int32) - send_row
    slot_rows = jnp.minimum(send_start[:, None] + slots[None, :], frames - 1)
    slot_used = slots[None, :] < send_row[:, None]
    outgoing = targets[slot_rows]
    out_mask = jnp.where(slot_used, valid[slot_rows], False).astype(jnp.bfloat16)
    incoming, in_mask = (
        lax.all_to_all(outgoing, "dp", split_axis=0, concat_axis=0, tiled=True),
        lax.all_to_all(out_mask, "dp", split_axis=0, concat_axis=0, tiled=True),
    )
    recv_end = jnp.cumsum(recv_col, dtype=jnp.int32)
    recv_start = recv_end - recv_col
    source_of = jnp.sum(
        (recv_end[None, :] <= positions[:, None]).astype(jnp.int32), axis=1, dtype=jnp.int32
    )
    select = jnp.arange(owner_count, dtype=jnp.int32)[None, :] == source_of[:, None]
    within = positions - jnp.sum(jnp.where(select, recv_start[None, :], 0), axis=1, dtype=jnp.int32)
    flat_slot = source_of * capacity + within
    target = incoming.reshape(owner_count * capacity, incoming.shape[2])[flat_slot]
    frame_mask = in_mask.reshape(owner_count * capacity)[flat_slot].astype(jnp.float32)
    full_in, full_out, full_head = (
        lax.all_gather(w_in, "dp", axis=0, tiled=True),
        lax.all_gather(w_out, "dp", axis=0, tiled=True),
        lax.all_gather(w_head, "dp", axis=0, tiled=True),
    )
    pre_act = jnp.dot(student_in, full_in, preferred_element_type=jnp.float32)
    activated = swoosh_low(pre_act).astype(jnp.bfloat16)
    features = (
        student_in.astype(jnp.float32)
        + jnp.dot(activated, full_out, preferred_element_type=jnp.float32)
    ).astype(jnp.bfloat16)
    predicted = jnp.dot(features, full_head, preferred_element_type=jnp.float32)
    err_grad = (
        (predicted - target.astype(jnp.float32)) * column_scale()[None, :] * frame_mask[:, None]
    ).astype(jnp.bfloat16)
    head_term = jnp.dot(features.T, err_grad, preferred_element_type=jnp.float32)
    feat_grad = jnp.dot(err_grad, full_head.T, preferred_element_type=jnp.float32).astype(
        jnp.bfloat16
    )
    out_term = jnp.dot(activated.T, feat_grad, preferred_element_type=jnp.float32)
    act_grad = jnp.dot(feat_grad, full_out.T, preferred_element_type=jnp.float32)
    pre_grad = (act_grad * swoosh_slope(pre_act)).astype(jnp.bfloat16)
    in_term = jnp.dot(student_in.T, pre_grad, preferred_element_type=jnp.float32)
    shards = (
        lax.psum_scatter(in_term, "dp", scatter_dimension=0, tiled=True),
        lax.psum_scatter(out_term, "dp", scatter_dimension=0, tiled=True),
        lax.psum_scatter(head_term, "dp", scatter_dimension=0, tiled=True),
    )
    grads = lax.psum((shards[0], shards[1], shards[2]), "teacher")
    return (grads[0], grads[1], grads[2])


def solution(mesh):
    in_specs = (
        P(("teacher", "dp"), None),
        P(("teacher", "dp"), None),
        P(("teacher", "dp"), None),
        P(None, "teacher"),
        P("teacher", None),
        P(None, "teacher"),
        P("teacher", None),
        P(None, "teacher"),
        P("teacher", None),
        P(("teacher", "dp")),
        P("teacher", None, None),
        P(("teacher", "dp"), None),
        P("dp", None),
        P("dp", None),
        P("dp", None),
    )
    out_specs = (P("dp", None), P("dp", None), P("dp", None))
    return jax.shard_map(body, mesh=mesh, in_specs=in_specs, out_specs=out_specs, check_vma=False)
```

profile of v0, /device:TPU:0, one launch (start us, length us, event | category | flops | bytes accessed | tf_op | source)
XLA Modules:
  0.0 560.5 jit_solution(7970248796661927803)
XLA Ops:
  17.3 17.4 %all_gather.22 = bf16[512,768]{1,0:T(8,128)(2,1)} all-gather(bf16[128,768]{1,0:T(8,128)(2,1)S(1)} %fusion.121), channel_id=1, replica_groups=mesh['teacher'=4,'dp'=32] {'teacher'}, dimensions={0}, use_global_device_ids=true | all-gather | bytes 983040 | tf_op jit(solution)/shard_map/all_gather | solution.py:65
  34.6 7.6 %fusion.108 = f32[512,768]{1,0:T(8,128)} fusion(bf16[768,768]{1,0:T(8,128)(2,1)} %param.25, bf16[512,768]{1,0:T(8,128)(2,1)} %all_gather.22, bf16[768,768]{1,0:T(8,128)(2,1)} %param.24), kind=kOutput, calls=%fused_computation.148 | convolution fusion | flops 1233518592 | bytes 4718592 | tf_op jit(solution)/shard_map/dot_general | solution.py:74
  42.2 10.1 %fusion.67 = f32[512,1024]{1,0:T(8,128)} fusion(bf16[1024,1024]{1,0:T(8,128)(2,1)} %param.27, bf16[512,1024]{1,0:T(8,128)(2,1)} %all-gather.14.cloned.1.call-done, bf16[1024,1024]{1,0:T(8,128)(2,1)} %param.26), kind=kOutput, calls=%fused_computation.105 | convolution fusion | flops 2181562368 | bytes 7340032 | tf_op jit(solution)/shard_map/dot_general | solution.py:74
  52.3 16.1 %all-gather.12.cloned.1.call-done = bf16[512,1280]{1,0:T(8,128)(2,1)} async-done(((bf16[128,1280]{1,0:T(8,128)(2,1)}), bf16[512,1280]{1,0:T(8,128)(2,1)}) %all-gather.12.cloned.1.call-update) | async-done | bytes 1310736 | tf_op jit(solution)/shard_map/all_gather | solution.py:64
  68.4 12.4 %fusion.34 = f32[512,1280]{1,0:T(8,128)} fusion(bf16[1280,1280]{1,0:T(8,128)(2,1)S(1)} %copy-done, bf16[512,1280]{1,0:T(8,128)(2,1)} %all-gather.12.cloned.1.call-done, bf16[1280,1280]{1,0:T(8,128)(2,1)} %param.22), kind=kOutput, calls=%fused_computation.71 | convolution fusion | flops 3398041600 | bytes 10485760 | tf_op jit(solution)/shard_map/dot_general | solution.py:74
  80.8 6.3 %pad_maximum_fusion = f32[512,3072]{1,0:T(8,128)} fusion(f32[512,1024]{1,0:T(8,128)} %fusion.67, f32[512,768]{1,0:T(8,128)} %fusion.108, f32[512,1280]{1,0:T(8,128)} %fusion.34), kind=kLoop, calls=%fused_computation.4 | loop fusion | flops 3145728 | bytes 12582912 | tf_op jit(solution)/shard_map/concatenate | solution.py:76
  94.2 7.4 %all-to-all-start.1 = ((bf16[32,1,8]{2,1,0:T(2,128)(2,1)}), bf16[32,1,8]{2,1,0:T(2,128)(2,1)}, u32[]{:S(2)}, u32[]{:S(2)}) async-start(bf16[32,1,8]{2,1,0:T(2,128)(2,1)} %copy.35), calls=%async_computation.2 | async-start | bytes 32768 | tf_op jit(solution)/shard_map/all_to_all | solution.py:95
  101.6 50.2 %reduce-scatter.7.cloned.1.call-done = f32[128,3072]{1,0:T(8,128)} async-done(((f32[512,3072]{1,0:T(8,128)}), f32[128,3072]{1,0:T(8,128)}) %reduce-scatter.7.cloned.1.call-update) | async-done | bytes 1572880 | tf_op jit(solution)/shard_map/reduce_scatter | solution.py:75
  154.4 5.5 gather_fusion
  160.0 7.5 %all-to-all-start = ((bf16[32,8,3072]{2,1,0:T(8,128)(2,1)}), bf16[32,8,3072]{2,1,0:T(8,128)(2,1)}, u32[]{:S(2)}, u32[]{:S(2)}) async-start(bf16[32,8,3072]{2,1,0:T(8,128)(2,1)} %bitcast.48), calls=%async_computation.1 | async-start | bytes 3145728 | tf_op jit(solution)/shard_map/all_to_all | solution.py:94
  170.5 2.7 fusion.236
  173.1 12.0 %all-gather.8.cloned.1.call-done = bf16[1536,512]{1,0:T(8,128)(2,1)} async-done(((bf16[48,512]{1,0:T(8,128)(2,1)}), bf16[1536,512]{1,0:T(8,128)(2,1)}) %all-gather.8.cloned.1.call-update) | async-done | bytes 1572880 | tf_op jit(solution)/shard_map/all_gather | solution.py:109
  187.5 4.8 all-to-all-done
  192.2 4.3 gather_fusion.1
  196.6 40.2 %all-gather.10.cloned.1.call-done = bf16[512,3072]{1,0:T(8,128)(2,1)} async-done(((bf16[16,3072]{1,0:T(8,128)(2,1)}), bf16[512,3072]{1,0:T(8,128)(2,1)}) %all-gather.10.cloned.1.call-update) | async-done | bytes 3145744 | tf_op jit(solution)/shard_map/all_gather | solution.py:110
  236.8 3.0 fusion.2
  241.9 4.4 convolution_bitcast_fusion
  246.3 3.6 copy.37
  250.0 3.6 fusion.225
  253.6 4.8 fusion.237
  258.5 71.2 %reduce-scatter.13.cloned.1.call-done = f32[16,1536]{1,0:T(8,128)} async-done(((f32[512,1536]{1,0:T(8,128)}), f32[16,1536]{1,0:T(8,128)}) %reduce-scatter.13.cloned.1.call-update) | async-done | bytes 98320
  331.7 81.7 %reduce-scatter.9.cloned.1.call-done = f32[48,512]{1,0:T(8,128)} async-done(((f32[1536,512]{1,0:T(8,128)}), f32[48,512]{1,0:T(8,128)}) %reduce-scatter.9.cloned.1.call-update) | async-done | bytes 98320 | tf_op jit(solution)/shard_map/reduce_scatter | solution.py:132
  413.4 89.3 %reduce-scatter.11.cloned.1.call-done = f32[16,3072]{1,0:T(8,128)} async-done(((f32[512,3072]{1,0:T(8,128)}), f32[16,3072]{1,0:T(8,128)}) %reduce-scatter.11.cloned.1.call-update) | async-done | bytes 196624 | tf_op jit(solution)/shard_map/reduce_scatter | solution.py:133
  502.7 45.5 %all-reduce.3.cloned.1.call-done = (f32[16,1536]{0,1:T(8,128)}, f32[48,512]{1,0:T(8,128)}, f32[16,3072]{1,0:T(8,128)}) async-done(((f32[16,1536]{0,1:T(8,128)}, f32[48,512]{1,0:T(8,128)}, f32[16,3072]{1,0:T(8,128)}), (f32[16,1536]{0,1:T(8,128)}, f32[48,512]{1,0:T(8,128)}, f32[16,3072]{1,0:T(8,128)})) %all-reduce.3.cloned.1.call-update) | async-done | bytes 393232 | tf_op jit(solution)/shard_map/psum | solution.py:135
  (87 shorter events, 32.8 us)
Async XLA Ops:
  8.0 60.4 %copy-start = (bf16[1280,1280]{1,0:T(8,128)(2,1)S(1)}, bf16[1280,1280]{1,0:T(8,128)(2,1)}, u32[]{:S(2)}) copy-start(bf16[1280,1280]{1,0:T(8,128)(2,1)} %param.23) | copy-start | bytes 9830404
  8.0 8.8 %copy-start.4 = (bf16[128,768]{1,0:T(8,128)(2,1)S(1)}, bf16[128,768]{1,0:T(8,128)(2,1)}, u32[]{:S(2)}) copy-start(bf16[128,768]{1,0:T(8,128)(2,1)} %param.20) | copy-start | bytes 589828
  8.0 34.2 %all-gather.14.cloned.1.call-start = ((), (), s32[]{:S(2)}) async-start(), calls=%async_computation.10 | async-start | bytes 1310720 | tf_op jit(solution)/shard_map/all_gather | solution.py:66
  12.4 56.0 %all-gather.12.cloned.1.call-start = ((), (), s32[]{:S(2)}) async-start(), calls=%async_computation.9 | async-start | bytes 1638400 | tf_op jit(solution)/shard_map/all_gather | solution.py:64
  16.7 135.1 %reduce-scatter.7.cloned.1.call-start = ((), (), s32[]{:S(2)}) async-start(), calls=%async_computation.11 | async-start | bytes 7864320 | tf_op jit(solution)/shard_map/reduce_scatter | solution.py:75
  87.2 83.3 %all-gather.6.cloned.1.call-start = ((), (), s32[]{:S(2)}) async-start(), calls=%async_computation.6 | async-start | bytes 1622016 | tf_op jit(solution)/shard_map/all_gather | solution.py:108
  87.8 97.4 %all-gather.8.cloned.1.call-start = ((), (), s32[]{:S(2)}) async-start(), calls=%async_computation.7 | async-start | bytes 1622016 | tf_op jit(solution)/shard_map/all_gather | solution.py:109
  88.4 148.4 %all-gather.10.cloned.1.call-start = ((), (), s32[]{:S(2)}) async-start(), calls=%async_computation.8 | async-start | bytes 3244032 | tf_op jit(solution)/shard_map/all_gather | solution.py:110
  91.4 60.4 %copy-start.3 = (bf16[128,1024]{1,0:T(8,128)(2,1)S(1)}, bf16[128,1024]{1,0:T(8,128)(2,1)}, u32[]{:S(2)}) copy-start(bf16[128,1024]{1,0:T(8,128)(2,1)} %param.21) | copy-start | bytes 786436
  94.2 65.7 %all-to-all-start.1 = ((bf16[32,1,8]{2,1,0:T(2,128)(2,1)}), bf16[32,1,8]{2,1,0:T(2,128)(2,1)}, u32[]{:S(2)}, u32[]{:S(2)}) async-start(bf16[32,1,8]{2,1,0:T(2,128)(2,1)} %copy.35), calls=%async_computation.2 | async-start | bytes 32768 | tf_op jit(solution)/shard_map/all_to_all | solution.py:95
  159.9 7.8 %copy-start.6 = (s32[1,32,32]{2,1,0:T(8,128)S(1)}, s32[1,32,32]{2,1,0:T(8,128)}, u32[]{:S(2)}) copy-start(s32[1,32,32]{2,1,0:T(8,128)} %param.29) | copy-start | bytes 12292
  159.9 10.5 %copy-start.5 = (bf16[128,512]{1,0:T(8,128)(2,1)S(1)}, bf16[128,512]{1,0:T(8,128)(2,1)}, u32[]{:S(2)}) copy-start(bf16[128,512]{1,0:T(8,128)(2,1)} %param.30) | copy-start | bytes 393220
  160.0 32.3 %all-to-all-start = ((bf16[32,8,3072]{2,1,0:T(8,128)(2,1)}), bf16[32,8,3072]{2,1,0:T(8,128)(2,1)}, u32[]{:S(2)}, u32[]{:S(2)}) async-start(bf16[32,8,3072]{2,1,0:T(8,128)(2,1)} %bitcast.48), calls=%async_computation.1 | async-start | bytes 3145728 | tf_op jit(solution)/shard_map/all_to_all | solution.py:94
  167.4 162.2 %reduce-scatter.13.cloned.1.call-start = ((), (), s32[]{:S(2)}) async-start(), calls=%async_computation.14 | async-start | bytes 3244032
  192.2 44.5 %copy-start.7 = (f32[3072]{0:T(1024)S(1)}, f32[3072]{0:T(1024)}, u32[]{:S(2)}) copy-start(f32[3072]{0:T(1024)} %constant.283.clone.1) | copy-start | bytes 36868
  236.8 3.9 copy-start.1
  239.8 0.9 copy-start.2
  249.9 163.5 %reduce-scatter.9.cloned.1.call-start = ((), (), s32[]{:S(2)}) async-start(), calls=%async_computation.12 | async-start | bytes 3244032 | tf_op jit(solution)/shard_map/reduce_scatter | solution.py:132
  253.6 249.1 %reduce-scatter.11.cloned.1.call-start = ((), (), s32[]{:S(2)}) async-start(), calls=%async_computation.13 | async-start | bytes 6488064 | tf_op jit(solution)/shard_map/reduce_scatter | solution.py:133
  258.4 289.7 %all-reduce.3.cloned.1.call-start = ((), (), s32[]{:S(2)}) async-start(), calls=%async_computation.15 | async-start | bytes 2162688 | tf_op jit(solution)/shard_map/psum | solution.py:135
Sparse Core Ops, SparseCore 0:
  12.5 28.0 all-gather.13
  42.3 26.1 all-gather.11
  87.3 64.5 reduce-scatter.6
  502.8 45.3 all-reduce.2
Sparse Core Ops, SparseCore 1:
  89.9 43.9 all-gather.5
  136.0 49.1 all-gather.7
  187.3 49.4 all-gather.9
  250.0 79.6 reduce-scatter.12
  333.8 79.6 reduce-scatter.8
  417.2 85.5 reduce-scatter.10
where the time goes:
time: 561 us; the launch traced here: 560 us
  waiting for transfers between devices  413 us (74%)
  matrix products  52 us (9%)
  local copies, waits for them, and re-layouts  26.8 us (5%)
  other arithmetic  20 us (4%)
  blocking collectives  17.4 us (3%)
  between operations  16.1 us (3%)
  starting transfers between devices  15.5 us (3%)
    reduce_scatter x1, waiting for transfers between devices, body(): lax.psum_scatter(head_term, 'dp', scatter_dimension=0, tiled=True)  89.3 us
    reduce_scatter x1, waiting for transfers between devices, body(): lax.psum_scatter(out_term, 'dp', scatter_dimension=0, tiled=True)  81.7 us
    unnamed x11, waiting for transfers between devices  72.9 us
    reduce_scatter x1, waiting for transfers between devices, body(): lax.psum_scatter(jnp.concatenate(pieces, axis=1), 'teacher', scatter_dime...  50.2 us
    psum x1, waiting for transfers between devices, body(): grads = lax.psum((shards[0], shards[1], shards[2]), 'teacher')  45.5 us
    all_gather x1, waiting for transfers between devices, body(): lax.all_gather(w_head, 'dp', axis=0, tiled=True)  40.2 us
    dot_general x3, matrix products, body(): jnp.dot(hidden, down_proj, preferred_element_type=jnp.float32)  30.1 us
    all_gather x1, blocking collectives, body(): lax.all_gather(normed_beats, 'teacher', axis=0, tiled=True)  17.4 us
  transfers between devices with their start and end apart: 12, of which 9 were waited for; matrix products, arithmetic and copies ran while one was open for 10% of the time, Pallas kernels for 0%

commit v1 on v0

--- a/solution.py
+++ b/solution.py
@@ -1,6 +1,8 @@
 import jax
 import jax.numpy as jnp
 from jax import lax
+from jax.experimental import pallas as pl
+from jax.experimental.pallas import tpu as pltpu
 from jax.sharding import PartitionSpec as P
 
 WH = 1280
@@ -34,6 +36,159 @@
             jnp.full((WL,), 2.0 / WL, jnp.float32),
         ]
     )
+
+
+GRAD_ROWS = 192
+MESH_ID = pl.DeviceIdType.MESH
+
+
+def grad_kernel(
+    in_t, act_t, feat_t, pre, fgrad, err, out,
+    lin, lact, lfeat, rpre, rfg, rerr,
+    own1, send1, recv1, send2, recv2, send3, recv3, mine3,
+    xs, xr, s1s, s1r, s2s, s2r, s3s, s3r, s4s, s4r,
+):
+    y = lax.axis_index("teacher")
+    dp = lax.axis_index("dp")
+    c = dp % 2
+    z = (dp // 2) % 4
+    x = dp // 8
+    swap = c == 1
+    first = jnp.where(swap, z, x)
+    second = jnp.where(swap, x, z)
+
+    def at_first(a):
+        return {"dp": jnp.where(swap, (x * 4 + a) * 2 + 1, (a * 4 + z) * 2)}
+
+    def at_second(b):
+        return {"dp": jnp.where(swap, (b * 4 + z) * 2 + 1, (x * 4 + b) * 2)}
+
+    def at_y(t):
+        return {"teacher": t}
+
+    pair = {"dp": (x * 4 + z) * 2 + (1 - c)}
+    barrier = pltpu.get_barrier_semaphore()
+    pl.semaphore_signal(barrier, inc=1, device_id=pair, device_id_type=MESH_ID)
+    for d in range(1, 4):
+        for dev in (at_first((first + d) % 4), at_second((second + d) % 4), at_y((y + d) % 4)):
+            pl.semaphore_signal(barrier, inc=1, device_id=dev, device_id_type=MESH_ID)
+    pl.semaphore_wait(barrier, 10)
+
+    swaps = []
+    for i, (src, dst) in enumerate((
+        (fgrad, rfg.at[pl.ds(128, 128)]),
+        (act_t.at[1 - c], lact.at[:, :, :, pl.ds(128, 128)]),
+        (in_t.at[1 - c], lin.at[:, :, :, pl.ds(128, 128)]),
+        (feat_t.at[1 - c], lfeat.at[:, :, :, pl.ds(128, 128)]),
+        (pre, rpre.at[pl.ds(128, 128)]),
+        (err, rerr.at[pl.ds(128, 128)]),
+    )):
+        cp = pltpu.make_async_remote_copy(
+            src_ref=src, dst_ref=dst, send_sem=xs.at[i], recv_sem=xr.at[i],
+            device_id=pair, device_id_type=MESH_ID)
+        cp.start()
+        swaps.append(cp)
+    lin[:, :, :, 0:128] = in_t[c]
+    lact[:, :, :, 0:128] = act_t[c]
+    lfeat[:, :, :, 0:128] = feat_t[c]
+    rpre[0:128] = pre[...]
+    rfg[0:128] = fgrad[...]
+    rerr[0:128] = err[...]
+    for cp in swaps:
+        cp.wait()
+
+    def block(a, store):
+        li = lin[a].reshape(64, 256)
+        lo = lact[a].reshape(192, 256)
+        lh = lfeat[a].reshape(64, 256)
+        for n in range(3):
+            v = jnp.dot(li, rpre[:, 512 * n:512 * n + 512], preferred_element_type=jnp.float32)
+            store(16 * n, 16, v.reshape(4, 16, 512))
+        v = jnp.dot(lo, rfg[...], preferred_element_type=jnp.float32)
+        store(48, 48, v.reshape(4, 48, 512))
+        for n in range(6):
+            v = jnp.dot(lh, rerr[:, 512 * n:512 * n + 512], preferred_element_type=jnp.float32)
+            store(96 + 16 * n, 16, v.reshape(4, 16, 512))
+
+    def send(src, dst, ssem, rsem, dev):
+        cp = pltpu.make_async_remote_copy(
+            src_ref=src, dst_ref=dst, send_sem=ssem, recv_sem=rsem,
+            device_id=dev, device_id_type=MESH_ID)
+        cp.start()
+        return cp
+
+    copies = {}
+    for d in (2, 1, 3):
+        a = (first + d) % 4
+
+        def put(r, h, v, d=d):
+            send1[d - 1, :, r:r + h, :] = v.astype(send1.dtype)
+        block(a, put)
+        copies[d] = send(send1.at[d - 1], recv1.at[d - 1], s1s.at[d - 1], s1r.at[d - 1], at_first(a))
+
+    def put_own(r, h, v):
+        own1[:, r:r + h, :] = v
+    block(first, put_own)
+    for d in (1, 3, 2):
+        copies[d].wait()
+
+    def total1(b):
+        return (own1[b] + recv1[0, b].astype(jnp.float32)
+                + recv1[1, b].astype(jnp.float32) + recv1[2, b].astype(jnp.float32))
+
+    for d in (2, 1, 3):
+        b = (second + d) % 4
+        send2[d - 1] = total1(b).astype(send2.dtype)
+        copies[d] = send(send2.at[d - 1], recv2.at[d - 1], s2s.at[d - 1], s2r.at[d - 1], at_second(b))
+    own2 = total1(second)
+    for d in (1, 3, 2):
+        copies[d].wait()
+    total = (own2 + recv2[0].astype(jnp.float32) + recv2[1].astype(jnp.float32)
+             + recv2[2].astype(jnp.float32))
+    send3[...] = total.reshape(4, 48, 512)
+    for d in (2, 1, 3):
+        t = (y + d) % 4
+        copies[d] = send(send3.at[t], recv3.at[d - 1], s3s.at[d - 1], s3r.at[d - 1], at_y(t))
+    for d in (1, 3, 2):
+        copies[d].wait()
+    final = send3[y] + recv3[0] + recv3[1] + recv3[2]
+    mine3[...] = final
+    out[y] = final
+    for d in (2, 1, 3):
+        t = (y + d) % 4
+        copies[d] = send(mine3, out.at[y], s4s.at[d - 1], s4r.at[d - 1], at_y(t))
+    for d in (1, 3, 2):
+        copies[d].wait()
+
+
+def reduce_grads(student_in, activated, features, pre_grad, feat_grad, err_grad):
+    def rows_of(values, h):
+        t = values.T.reshape(4, 4, 2, h, values.shape[0])
+        return jnp.stack([t[:, :, 0], t[:, :, 1].transpose(1, 0, 2, 3)])
+
+    bf, f32 = jnp.bfloat16, jnp.float32
+    vm = pl.BlockSpec(memory_space=pltpu.VMEM)
+    dma = pltpu.SemaphoreType.DMA
+    g = GRAD_ROWS
+    out = pl.pallas_call(
+        grad_kernel,
+        out_shape=jax.ShapeDtypeStruct((4, 48, 512), f32),
+        in_specs=[vm] * 6,
+        out_specs=vm,
+        scratch_shapes=[
+            pltpu.VMEM((4, 4, 16, 256), bf), pltpu.VMEM((4, 4, 48, 256), bf), pltpu.VMEM((4, 4, 16, 256), bf),
+            pltpu.VMEM((256, 1536), bf), pltpu.VMEM((256, 512), bf), pltpu.VMEM((256, 3072), bf),
+            pltpu.VMEM((4, g, 512), f32), pltpu.VMEM((3, 4, g, 512), bf), pltpu.VMEM((3, 4, g, 512), bf),
+            pltpu.VMEM((3, g, 512), bf), pltpu.VMEM((3, g, 512), bf),
+            pltpu.VMEM((4, 48, 512), f32), pltpu.VMEM((3, 48, 512), f32), pltpu.VMEM((48, 512), f32),
+            dma((6,)), dma((6,)), dma((3,)), dma((3,)), dma((3,)), dma((3,)), dma((3,)), dma((3,)), dma((3,)), dma((3,)),
+        ],
+        compiler_params=pltpu.CompilerParams(
+            collective_id=0, has_side_effects=True, vmem_limit_bytes=40 * 1024 * 1024),
+    )(rows_of(student_in, 16), rows_of(activated, 48), rows_of(features, 16), pre_grad, feat_grad, err_grad)
+    flat = out.reshape(g, 512)
+    wide = lambda v, n: v.reshape(n, 16, 512).transpose(1, 0, 2).reshape(16, n * 512)
+    return wide(flat[0:48], 3), flat[48:96], wide(flat[96:192], 6)
 
 
 def body(
@@ -119,21 +274,12 @@
     err_grad = (
         (predicted - target.astype(jnp.float32)) * column_scale()[None, :] * frame_mask[:, None]
     ).astype(jnp.bfloat16)
-    head_term = jnp.dot(features.T, err_grad, preferred_element_type=jnp.float32)
     feat_grad = jnp.dot(err_grad, full_head.T, preferred_element_type=jnp.float32).astype(
         jnp.bfloat16
     )
-    out_term = jnp.dot(activated.T, feat_grad, preferred_element_type=jnp.float32)
     act_grad = jnp.dot(feat_grad, full_out.T, preferred_element_type=jnp.float32)
     pre_grad = (act_grad * swoosh_slope(pre_act)).astype(jnp.bfloat16)
-    in_term = jnp.dot(student_in.T, pre_grad, preferred_element_type=jnp.float32)
-    shards = (
-        lax.psum_scatter(in_term, "dp", scatter_dimension=0, tiled=True),
-        lax.psum_scatter(out_term, "dp", scatter_dimension=0, tiled=True),
-        lax.psum_scatter(head_term, "dp", scatter_dimension=0, tiled=True),
-    )
-    grads = lax.psum((shards[0], shards[1], shards[2]), "teacher")
-    return (grads[0], grads[1], grads[2])
+    return reduce_grads(student_in, activated, features, pre_grad, feat_grad, err_grad)
 
 
 def solution(mesh):

time: 561 us -> 300 us (0.53)
  waiting for transfers between devices: 413 us -> 110 us
  Pallas kernels: 0 us -> 46.4 us
  matrix products: 52 us -> 40.4 us
    reduce_scatter x2 -> x0, waiting for transfers between devices: 171 us -> none  [the longest x1 89.3 us: body(): lax.psum_scatter(head_term, 'dp', scatter_dimension=0, tiled=True)]
    unnamed x11 -> x6, waiting for transfers between devices: 72.9 us -> 1.62 us
    pallas_call x0 -> x1, Pallas kernels: none -> 46.4 us  [reduce_grads(): pl.pallas_call(grad_kernel, out_shape=jax.ShapeDtypeStruct((4, 48, 512),...]
    psum x1 -> x0, waiting for transfers between devices: 45.5 us -> none  [body(): grads = lax.psum((shards[0], shards[1], shards[2]), 'teacher')]
    dot_general x3 -> x1, matrix products: 12.8 us -> 0.65 us  [body(): jnp.dot(feat_grad, full_out.T, preferred_element_type=jnp.float32)]
    unnamed x21 -> x28, local copies, waits for them, and re-layouts: 11.8 us -> 4.56 us
    reduce_scatter x1, waiting for transfers between devices: 50.2 us -> 43.2 us  [body(): lax.psum_scatter(jnp.concatenate(pieces, axis=1), 'teacher', scatter_dime...]
  transfers between devices with their start and end apart: 12 -> 8, of which waited for: 9 -> 4; matrix products, arithmetic and copies ran while one was open for 10% -> 21% of each run, Pallas kernels for 0% -> 0%
where the time goes in v1:
time: 300 us; the launch traced here: 298 us
  waiting for transfers between devices  110 us (37%)
  Pallas kernels  46.4 us (15%)
  matrix products  40.4 us (13%)
  local copies, waits for them, and re-layouts  28.4 us (9%)
  other arithmetic  24.3 us (8%)
  blocking collectives  17.4 us (6%)
  between operations  16.3 us (5%)
  starting transfers between devices  15.3 us (5%)
    pallas_call x1, Pallas kernels, reduce_grads(): pl.pallas_call(grad_kernel, out_shape=jax.ShapeDtypeStruct((4, 48, 512),...  46.4 us
    reduce_scatter x1, waiting for transfers between devices, body(): lax.psum_scatter(jnp.concatenate(pieces, axis=1), 'teacher', scatter_dime...  43.2 us
    all_gather x1, waiting for transfers between devices, body(): lax.all_gather(w_head, 'dp', axis=0, tiled=True)  37.4 us
    dot_general x3, matrix products, body(): jnp.dot(hidden, down_proj, preferred_element_type=jnp.float32)  30.1 us
    all_gather x1, blocking collectives, body(): lax.all_gather(normed_beats, 'teacher', axis=0, tiled=True)  17.4 us
    all_gather x1, waiting for transfers between devices, body(): lax.all_gather(normed_whisper, 'teacher', axis=0, tiled=True)  16.1 us
    all_gather x1, waiting for transfers between devices, body(): lax.all_gather(w_out, 'dp', axis=0, tiled=True)  11.6 us
    all_to_all x1, starting transfers between devices, body(): lax.all_to_all(outgoing, 'dp', split_axis=0, concat_axis=0, tiled=True)  7.7 us
  transfers between devices with their start and end apart: 8, of which 4 were waited for; matrix products, arithmetic and copies ran while one was open for 21% of the time, Pallas kernels for 0%

profile of v1, /device:TPU:0, one launch (start us, length us, event | category | flops | bytes accessed | tf_op | source)
XLA Modules:
  0.0 298.4 jit_solution(14299897189809894623)
XLA Ops:
  10.5 1.9 fusion.118
  14.8 1.9 fusion.114
  17.3 17.4 %all_gather.22 = bf16[512,768]{1,0:T(8,128)(2,1)} all-gather(bf16[128,768]{1,0:T(8,128)(2,1)S(1)} %fusion.122), channel_id=1, replica_groups=mesh['teacher'=4,'dp'=32] {'teacher'}, dimensions={0}, use_global_device_ids=true | all-gather | bytes 983040 | tf_op jit(solution)/shard_map/all_gather | solution.py:220
  34.6 7.6 %fusion.109 = f32[512,768]{1,0:T(8,128)} fusion(bf16[768,768]{1,0:T(8,128)(2,1)} %param.25, bf16[512,768]{1,0:T(8,128)(2,1)} %all_gather.22, bf16[768,768]{1,0:T(8,128)(2,1)} %param.24), kind=kOutput, calls=%fused_computation.150 | convolution fusion | flops 1233518592 | bytes 4718592 | tf_op jit(solution)/shard_map/dot_general | solution.py:229
  42.2 10.1 %fusion.67 = f32[512,1024]{1,0:T(8,128)} fusion(bf16[1024,1024]{1,0:T(8,128)(2,1)} %param.27, bf16[512,1024]{1,0:T(8,128)(2,1)} %all-gather.14.cloned.1.call-done, bf16[1024,1024]{1,0:T(8,128)(2,1)} %param.26), kind=kOutput, calls=%fused_computation.105 | convolution fusion | flops 2181562368 | bytes 7340032 | tf_op jit(solution)/shard_map/dot_general | solution.py:229
  52.3 16.1 %all-gather.12.cloned.1.call-done = bf16[512,1280]{1,0:T(8,128)(2,1)} async-done(((bf16[128,1280]{1,0:T(8,128)(2,1)}), bf16[512,1280]{1,0:T(8,128)(2,1)}) %all-gather.12.cloned.1.call-update) | async-done | bytes 1310736 | tf_op jit(solution)/shard_map/all_gather | solution.py:219
  68.4 12.4 %fusion.34 = f32[512,1280]{1,0:T(8,128)} fusion(bf16[1280,1280]{1,0:T(8,128)(2,1)S(1)} %copy-done, bf16[512,1280]{1,0:T(8,128)(2,1)} %all-gather.12.cloned.1.call-done, bf16[1280,1280]{1,0:T(8,128)(2,1)} %param.22), kind=kOutput, calls=%fused_computation.71 | convolution fusion | flops 3398041600 | bytes 10485760 | tf_op jit(solution)/shard_map/dot_general | solution.py:229
  80.8 6.3 %pad_maximum_fusion = f32[512,3072]{1,0:T(8,128)} fusion(f32[512,1024]{1,0:T(8,128)} %fusion.67, f32[512,768]{1,0:T(8,128)} %fusion.109, f32[512,1280]{1,0:T(8,128)} %fusion.34), kind=kLoop, calls=%fused_computation.4 | loop fusion | flops 3145728 | bytes 12582912 | tf_op jit(solution)/shard_map/concatenate | solution.py:231
  91.5 1.9 gather_fusion.2
  94.2 7.4 %all-to-all-start.1 = ((bf16[32,1,8]{2,1,0:T(2,128)(2,1)}), bf16[32,1,8]{2,1,0:T(2,128)(2,1)}, u32[]{:S(2)}, u32[]{:S(2)}) async-start(bf16[32,1,8]{2,1,0:T(2,128)(2,1)} %copy.79), calls=%async_computation.2 | async-start | bytes 32768 | tf_op jit(solution)/shard_map/all_to_all | solution.py:250
  105.3 1.7 copy.67
  107.2 1.5 slice_bitcast_fusion.3
  108.7 43.2 %reduce-scatter.2.cloned.1.call-done = f32[128,3072]{1,0:T(8,128)} async-done(((f32[512,3072]{1,0:T(8,128)}), f32[128,3072]{1,0:T(8,128)}) %reduce-scatter.2.cloned.1.call-update) | async-done | bytes 1572880 | tf_op jit(solution)/shard_map/reduce_scatter | solution.py:230
  151.9 2.6 add_convert_fusion
  154.4 5.5 %gather_fusion = bf16[256,3072]{1,0:T(8,128)(2,1)} fusion(bf16[128,3072]{1,0:T(8,128)(2,1)} %add_convert_fusion, s32[1024]{0:T(1024)S(1)} %pad_clamp_fusion.1), kind=kCustom, calls=%fused_computation | custom fusion | bytes 3146752 | tf_op jit(solution)/shard_map/gather | solution.py:246
  160.0 7.7 %all-to-all-start = ((bf16[32,8,3072]{2,1,0:T(8,128)(2,1)}), bf16[32,8,3072]{2,1,0:T(8,128)(2,1)}, u32[]{:S(2)}, u32[]{:S(2)}) async-start(bf16[32,8,3072]{2,1,0:T(8,128)(2,1)} %bitcast.110), calls=%async_computation.1 | async-start | bytes 3145728 | tf_op jit(solution)/shard_map/all_to_all | solution.py:249
  170.5 3.2 %fusion.101 = (bf16[1536,128]{0,1:T(8,128)(2,1)}, f32[128,1536]{1,0:T(8,128)}) fusion(bf16[128,512]{1,0:T(8,128)(2,1)} %param.30, bf16[512,1536]{1,0:T(8,128)(2,1)} %all-gather.6.cloned.1.call-done), kind=kOutput, calls=%fused_computation.140 | convolution fusion | flops 203489280 | bytes 2883584 | tf_op jit(solution)/shard_map/dot_general | solution.py:267
  173.6 11.6 %all-gather.8.cloned.1.call-done = bf16[1536,512]{1,0:T(8,128)(2,1)} async-done(((bf16[48,512]{1,0:T(8,128)(2,1)}), bf16[1536,512]{1,0:T(8,128)(2,1)}) %all-gather.8.cloned.1.call-update) | async-done | bytes 1572880 | tf_op jit(solution)/shard_map/all_gather | solution.py:264
  185.2 2.3 fusion.66
  190.4 1.9 copy.70
  195.1 4.3 %gather_fusion.1 = bf16[128,3072]{1,0:T(8,128)(2,1)} fusion(bf16[256,3072]{1,0:T(8,128)(2,1)} %bitcast.23, s32[1024]{0:T(1024)S(1)} %pad_clamp_fusion), kind=kCustom, calls=%fused_computation.1 | custom fusion | bytes 1573376 | tf_op jit(solution)/shard_map/gather | solution.py:260
  199.4 37.4 %all-gather.10.cloned.1.call-done = bf16[512,3072]{1,0:T(8,128)(2,1)} async-done(((bf16[16,3072]{1,0:T(8,128)(2,1)}), bf16[512,3072]{1,0:T(8,128)(2,1)}) %all-gather.10.cloned.1.call-update) | async-done | bytes 3145744 | tf_op jit(solution)/shard_map/all_gather | solution.py:265
  236.8 3.0 %fusion.2.err = bf16[128,3072]{1,0:T(8,128)(2,1)S(1)} fusion(bf16[128,512]{1,0:T(8,128)(2,1)} %copy-done.5, bf16[512,3072]{1,0:T(8,128)(2,1)} %all-gather.10.cloned.1.call-done, bf16[128,3072]{1,0:T(8,128)(2,1)} %gather_fusion.1, f32[128]{0:T(128)} %convert_element_type.95, f32[3072]{0:T(1024)S(1)} %copy-done.8), kind=kOutput, calls=%fused_computation.9 | convolution fusion | flops 404619264 | bytes 4862464 | tf_op jit(solution)/shard_map/dot_general | solution.py:273
  242.6 46.4 %shard_map.169 = f32[4,48,512]{2,1,0:T(8,128)S(1)} custom-call(bf16[2,4,4,16,128]{4,3,2,1,0:T(8,128)(2,1)S(1)} %pad_maximum_fusion.2.in_t, bf16[2,4,4,48,128]{4,3,2,1,0:T(8,128)(2,1)S(1)} %copy-done.1, bf16[2,4,4,16,128]{4,3,2,1,0:T(8,128)(2,1)S(1)} %pad_maximum_fusion.3.feat_t, bf16[128,1536]{1,0:T(8,128)(2,1)S(1)} %fusion.13.pre, ...), custom_call_target="tpu_custom_call" | custom-call | tf_op jit(solution)/shard_map/pallas_call | solution.py:173
  (92 shorter events, 26.9 us)
Async XLA Ops:
  8.0 60.4 %copy-start = (bf16[1280,1280]{1,0:T(8,128)(2,1)S(1)}, bf16[1280,1280]{1,0:T(8,128)(2,1)}, u32[]{:S(2)}) copy-start(bf16[1280,1280]{1,0:T(8,128)(2,1)} %param.23) | copy-start | bytes 9830404
  8.0 8.8 %copy-start.4 = (bf16[128,768]{1,0:T(8,128)(2,1)S(1)}, bf16[128,768]{1,0:T(8,128)(2,1)}, u32[]{:S(2)}) copy-start(bf16[128,768]{1,0:T(8,128)(2,1)} %param.20) | copy-start | bytes 589828
  8.0 34.2 %all-gather.14.cloned.1.call-start = ((), (), s32[]{:S(2)}) async-start(), calls=%async_computation.7 | async-start | bytes 1310720 | tf_op jit(solution)/shard_map/all_gather | solution.py:221
  12.4 56.0 %all-gather.12.cloned.1.call-start = ((), (), s32[]{:S(2)}) async-start(), calls=%async_computation.6 | async-start | bytes 1638400 | tf_op jit(solution)/shard_map/all_gather | solution.py:219
  16.7 135.1 %reduce-scatter.2.cloned.1.call-start = ((), (), s32[]{:S(2)}) async-start(), calls=%async_computation.8 | async-start | bytes 7864320 | tf_op jit(solution)/shard_map/reduce_scatter | solution.py:230
  87.2 83.3 %all-gather.6.cloned.1.call-start = ((), (), s32[]{:S(2)}) async-start(), calls=%async_computation.3 | async-start | bytes 1622016 | tf_op jit(solution)/shard_map/all_gather | solution.py:263
  87.8 97.4 %all-gather.8.cloned.1.call-start = ((), (), s32[]{:S(2)}) async-start(), calls=%async_computation.4 | async-start | bytes 1622016 | tf_op jit(solution)/shard_map/all_gather | solution.py:264
  88.4 148.5 %all-gather.10.cloned.1.call-start = ((), (), s32[]{:S(2)}) async-start(), calls=%async_computation.5 | async-start | bytes 3244032 | tf_op jit(solution)/shard_map/all_gather | solution.py:265
  91.4 60.4 %copy-start.3 = (bf16[128,1024]{1,0:T(8,128)(2,1)S(1)}, bf16[128,1024]{1,0:T(8,128)(2,1)}, u32[]{:S(2)}) copy-start(bf16[128,1024]{1,0:T(8,128)(2,1)} %param.21) | copy-start | bytes 786436
  94.2 65.7 %all-to-all-start.1 = ((bf16[32,1,8]{2,1,0:T(2,128)(2,1)}), bf16[32,1,8]{2,1,0:T(2,128)(2,1)}, u32[]{:S(2)}, u32[]{:S(2)}) async-start(bf16[32,1,8]{2,1,0:T(2,128)(2,1)} %copy.79), calls=%async_computation.2 | async-start | bytes 32768 | tf_op jit(solution)/shard_map/all_to_all | solution.py:250
  160.0 7.7 %copy-start.6 = (bf16[4,4,1,16,128]{4,3,2,1,0:T(8,128)(2,1)S(1)}, bf16[4,4,1,16,128]{4,3,2,1,0:T(8,128)(2,1)}, u32[]{:S(2)}) copy-start(bf16[4,4,1,16,128]{4,3,2,1,0:T(8,128)(2,1)} %get-tuple-element.36) | copy-start | bytes 196612
  160.0 7.8 %copy-start.7 = (bf16[1,4,4,16,128]{4,3,2,1,0:T(8,128)(2,1)S(1)}, bf16[1,4,4,16,128]{4,3,2,1,0:T(8,128)(2,1)}, u32[]{:S(2)}) copy-start(bf16[1,4,4,16,128]{4,3,2,1,0:T(8,128)(2,1)} %get-tuple-element.35) | copy-start | bytes 196612
  160.0 35.1 %all-to-all-start = ((bf16[32,8,3072]{2,1,0:T(8,128)(2,1)}), bf16[32,8,3072]{2,1,0:T(8,128)(2,1)}, u32[]{:S(2)}, u32[]{:S(2)}) async-start(bf16[32,8,3072]{2,1,0:T(8,128)(2,1)} %bitcast.110), calls=%async_computation.1 | async-start | bytes 3145728 | tf_op jit(solution)/shard_map/all_to_all | solution.py:249
  187.5 5.9 %copy-start.5 = (bf16[128,512]{1,0:T(8,128)(2,1)}, bf16[128,512]{1,0:T(8,128)(2,1)S(1)}, u32[]{:S(2)}) copy-start(bf16[128,512]{1,0:T(8,128)(2,1)S(1)} %fusion.66) | copy-start | bytes 393220
  195.1 41.8 %copy-start.8 = (f32[3072]{0:T(1024)S(1)}, f32[3072]{0:T(1024)}, u32[]{:S(2)}) copy-start(f32[3072]{0:T(1024)} %constant.283.clone.1) | copy-start | bytes 36868
  236.8 3.1 %copy-start.2 = (bf16[512,3072]{1,0:T(8,128)(2,1)S(1)}, bf16[512,3072]{1,0:T(8,128)(2,1)}, u32[]{:S(2)}) copy-start(bf16[512,3072]{1,0:T(8,128)(2,1)} %all-gather.10.cloned.1.call-done) | copy-start | bytes 9437188
  240.0 1.4 copy-start.9
  240.0 1.6 copy-start.10
  241.6 1.0 copy-start.1
Sparse Core Ops, SparseCore 0:
  12.5 28.0 all-gather.13
  42.3 26.1 all-gather.11
  87.3 64.5 reduce-scatter.1
Sparse Core Ops, SparseCore 1:
  89.9 43.9 all-gather.5
  136.0 49.2 all-gather.7
  187.3 49.4 all-gather.9

commit v2 on v1

--- a/solution.py
+++ b/solution.py
@@ -191,6 +191,199 @@
     return wide(flat[0:48], 3), flat[48:96], wide(flat[96:192], 6)
 
 
+TEACHERS = ((2, WL, WH + WB), (0, WH, 0), (1, WB, WH))
+
+
+def gelu(values):
+    return 0.5 * values * (1.0 + lax.erf(values * 0.7071067811865476))
+
+
+def teacher_kernel(*refs):
+    hid = refs[0:3]
+    ups, downs = refs[3:9:2], refs[4:9:2]
+    shards = refs[9:12]
+    targets = refs[12]
+    full = refs[13:16]
+    scratch = refs[16:]
+    vup, vdown, normed, keep, part, sopp, ropp, sside, rside = (scratch[3 * i:3 * i + 3] for i in range(9))
+    hidden, wsem, ags, agr, fws, fwr, ops_, opr, sds, sdr, w1s, w1r, w2s, w2r, w3s, w3r = scratch[27:]
+    y = lax.axis_index("teacher")
+    dp = lax.axis_index("dp")
+    c = dp % 2
+    z = (dp // 2) % 4
+    x = dp // 8
+    swap = c == 1
+    first = jnp.where(swap, z, x)
+    second = jnp.where(swap, x, z)
+    right, left = {"teacher": (y + 1) % 4}, {"teacher": (y + 3) % 4}
+    pair = {"dp": (x * 4 + z) * 2 + (1 - c)}
+
+    def at_first(a):
+        return {"dp": jnp.where(swap, (x * 4 + a) * 2 + 1, (a * 4 + z) * 2)}
+
+    def at_second(b):
+        return {"dp": jnp.where(swap, (b * 4 + z) * 2 + 1, (x * 4 + b) * 2)}
+
+    loads = {}
+    for n, (k, _, _) in enumerate(TEACHERS):
+        loads[k] = (pltpu.make_async_copy(ups[k], vup[k], wsem.at[2 * n]),
+                    pltpu.make_async_copy(downs[k], vdown[k], wsem.at[2 * n + 1]))
+        for cp in loads[k]:
+            cp.start()
+
+    barrier = pltpu.get_barrier_semaphore()
+    for dev in (right, left, pair):
+        pl.semaphore_signal(barrier, inc=1, device_id=dev, device_id_type=MESH_ID)
+    for d in range(1, 4):
+        for dev in (at_first((first + d) % 4), at_second((second + d) % 4)):
+            pl.semaphore_signal(barrier, inc=1, device_id=dev, device_id_type=MESH_ID)
+    for k in range(3):
+        normed[k][0] = layer_norm(hid[k][...]).astype(jnp.bfloat16)
+    for k in range(3):
+        full[k][x, z, c] = shards[k][...]
+    pl.semaphore_wait(barrier, 9)
+
+    def send(src, dst, ssem, rsem, dev):
+        cp = pltpu.make_async_remote_copy(
+            src_ref=src, dst_ref=dst, send_sem=ssem, recv_sem=rsem,
+            device_id=dev, device_id_type=MESH_ID)
+        cp.start()
+        return cp
+
+    def gather_out(k):
+        return (send(normed[k].at[0], normed[k].at[1], ags.at[k, 0], agr.at[k, 0], right),
+                send(normed[k].at[0], normed[k].at[2], ags.at[k, 1], agr.at[k, 1], left))
+
+    def forward(k):
+        lo, hi = pl.ds(0, 64), pl.ds(64, 64)
+        return (send(normed[k].at[1, lo], normed[k].at[3, lo], fws.at[k, 0], fwr.at[k, 0], right),
+                send(normed[k].at[2, hi], normed[k].at[3, hi], fws.at[k, 1], fwr.at[k, 1], left))
+
+    def ffn(k, width, slot, count, store):
+        rows = count * 128
+
+        def up_tile(j, carry):
+            cols = pl.ds(pl.multiple_of(j * 256, 256), 256)
+            values = normed[k][slot:slot + count].reshape(rows, width)
+            wide = jnp.dot(values, vup[k][:, cols], preferred_element_type=jnp.float32)
+            hidden[0:rows, cols] = gelu(wide).astype(jnp.bfloat16)
+            return carry
+
+        def down_tile(j, carry):
+            cols = pl.ds(pl.multiple_of(j * 256, 256), 256)
+            store(cols, jnp.dot(hidden[0:rows, 0:width], vdown[k][:, cols], preferred_element_type=jnp.float32))
+            return carry
+
+        lax.fori_loop(0, width // 256, up_tile, 0)
+        lax.fori_loop(0, width // 256, down_tile, 0)
+
+    order = [k for k, _, _ in TEACHERS]
+    gathers = {order[0]: gather_out(order[0])}
+    stage1 = []
+    for d in (2, 1, 3):
+        for m in range(3):
+            stage1.append(send(shards[m], full[m].at[x, z, c], w1s.at[d - 1, m], w1r.at[d - 1, m],
+                               at_first((first + d) % 4)))
+    gathers[order[1]] = gather_out(order[1])
+    stage2, stage3 = [], []
+
+    def weights_second():
+        for cp in stage1:
+            cp.wait()
+        for d in (2, 1, 3):
+            dev = at_second((second + d) % 4)
+            for m in range(3):
+                for i in range(4):
+                    slot = full[m].at[jnp.where(swap, x, i), jnp.where(swap, i, z), c]
+                    stage2.append(send(slot, slot, w2s.at[d - 1, m, i], w2r.at[d - 1, m, i], dev))
+
+    def weights_third():
+        for cp in stage2:
+            cp.wait()
+        for m in range(3):
+            half = full[m].at[:, :, c]
+            stage3.append(send(half, half, w3s.at[m], w3r.at[m], pair))
+
+    opposite, sides = {}, {}
+
+    def send_sides(k):
+        for cp in opposite[k]:
+            cp.wait()
+        sside[k][0, 0:64] = part[k][0, 0:64].astype(jnp.bfloat16)
+        sside[k][0, 64:128] = (part[k][0, 64:128] + ropp[k][1].astype(jnp.float32)).astype(jnp.bfloat16)
+        sside[k][1, 0:64] = (part[k][1, 0:64] + ropp[k][0].astype(jnp.float32)).astype(jnp.bfloat16)
+        sside[k][1, 64:128] = part[k][1, 64:128].astype(jnp.bfloat16)
+        sides[k] = (send(sside[k].at[1], rside[k].at[0], sds.at[k, 0], sdr.at[k, 0], right),
+                    send(sside[k].at[0], rside[k].at[1], sds.at[k, 1], sdr.at[k, 1], left))
+
+    for n, (k, width, _) in enumerate(TEACHERS):
+        for cp in loads[k]:
+            cp.wait()
+
+        def put_keep(cols, v):
+            keep[k][:, cols] = v
+        ffn(k, width, 0, 1, put_keep)
+        for cp in gathers[k]:
+            cp.wait()
+        passed = forward(k)
+        if n + 2 < 3:
+            gathers[order[n + 2]] = gather_out(order[n + 2])
+        if n > 0:
+            send_sides(order[n - 1])
+
+        def put_part(cols, v):
+            part[k][:, :, cols] = v.reshape(2, 128, 256)
+        ffn(k, width, 1, 2, put_part)
+        for cp in passed:
+            cp.wait()
+
+        def put_opp(cols, v):
+            sopp[k][:, :, cols] = v.astype(jnp.bfloat16).reshape(2, 64, 256)
+        ffn(k, width, 3, 1, put_opp)
+        opposite[k] = (send(sopp[k].at[0], ropp[k].at[0], ops_.at[k, 0], opr.at[k, 0], right),
+                       send(sopp[k].at[1], ropp[k].at[1], ops_.at[k, 1], opr.at[k, 1], left))
+        if n == 0:
+            weights_second()
+        if n == 1:
+            weights_third()
+    send_sides(order[2])
+    for k, width, start in TEACHERS:
+        for cp in sides[k]:
+            cp.wait()
+        total = (hid[k][...].astype(jnp.float32) + keep[k][...]
+                 + rside[k][0].astype(jnp.float32) + rside[k][1].astype(jnp.float32))
+        targets[:, start:start + width] = total.astype(jnp.bfloat16)
+    for cp in stage3:
+        cp.wait()
+
+
+def teacher_targets(hid, ups, downs, shards):
+    bf, f32 = jnp.bfloat16, jnp.float32
+    vm = pl.BlockSpec(memory_space=pltpu.VMEM)
+    hbm = pl.BlockSpec(memory_space=pl.ANY)
+    dma = pltpu.SemaphoreType.DMA
+    widths = (WH, WB, WL)
+    each = lambda shape, kind: [pltpu.VMEM(shape(w), kind) for w in widths]
+    pairs = [m for up_down in zip(ups, downs) for m in up_down]
+    outs = pl.pallas_call(
+        teacher_kernel,
+        out_shape=[jax.ShapeDtypeStruct((128, 3072), bf)]
+        + [jax.ShapeDtypeStruct((4, 4, 2) + s.shape, bf) for s in shards],
+        in_specs=[vm] * 3 + [hbm] * 6 + [vm] * 3,
+        out_specs=[vm] * 4,
+        scratch_shapes=each(lambda w: (w, w), bf) + each(lambda w: (w, w), bf)
+        + each(lambda w: (4, 128, w), bf) + each(lambda w: (128, w), f32) + each(lambda w: (2, 128, w), f32)
+        + each(lambda w: (2, 64, w), bf) + each(lambda w: (2, 64, w), bf)
+        + each(lambda w: (2, 128, w), bf) + each(lambda w: (2, 128, w), bf)
+        + [pltpu.VMEM((256, WH), bf), dma((6,))]
+        + [dma((3, 2))] * 8
+        + [dma((3, 3))] * 2 + [dma((3, 3, 4))] * 2 + [dma((3,))] * 2,
+        compiler_params=pltpu.CompilerParams(
+            collective_id=1, has_side_effects=True, vmem_limit_bytes=56 * 1024 * 1024),
+    )(*hid, *pairs, *shards)
+    return outs[0], [o.reshape(-1, o.shape[-1]) for o in outs[1:]]
+
+
 def body(
     hid_whisper,
     hid_beats,
@@ -212,62 +405,39 @@
     owner_index = lax.axis_index("dp")
     frames = hid_whisper.shape[0]
     capacity = 2 * frames // owner_count
-    normed_whisper = layer_norm(hid_whisper).astype(jnp.bfloat16)
-    normed_beats = layer_norm(hid_beats).astype(jnp.bfloat16)
-    normed_wavlm = layer_norm(hid_wavlm).astype(jnp.bfloat16)
-    gathered = (
-        lax.all_gather(normed_whisper, "teacher", axis=0, tiled=True),
-        lax.all_gather(normed_beats, "teacher", axis=0, tiled=True),
-        lax.all_gather(normed_wavlm, "teacher", axis=0, tiled=True),
-    )
-    pairs = ((up_whisper, down_whisper), (up_beats, down_beats), (up_wavlm, down_wavlm))
-    pieces = []
-    for rows_all, (up_proj, down_proj) in zip(gathered, pairs):
-        hidden = jax.nn.gelu(
-            jnp.dot(rows_all, up_proj, preferred_element_type=jnp.float32), approximate=False
-        ).astype(jnp.bfloat16)
-        pieces.append(jnp.dot(hidden, down_proj, preferred_element_type=jnp.float32))
-    summed = lax.psum_scatter(
-        jnp.concatenate(pieces, axis=1), "teacher", scatter_dimension=0, tiled=True
-    )
-    residual = jnp.concatenate([hid_whisper, hid_beats, hid_wavlm], axis=1).astype(jnp.float32)
-    targets = (summed + residual).astype(jnp.bfloat16)
     positions = jnp.arange(frames, dtype=jnp.int32)
     clip_slots = frames // clip_len.shape[0]
     lengths = jnp.repeat(clip_len, clip_slots, total_repeat_length=frames)
-    valid = positions % clip_slots < lengths
+    frame_mask = (positions % clip_slots < lengths).astype(jnp.float32)
     table = send_counts[0]
     send_row = lax.dynamic_index_in_dim(table, owner_index, 0, keepdims=False)
     recv_col = lax.dynamic_index_in_dim(table, owner_index, 1, keepdims=False)
     slots = jnp.arange(capacity, dtype=jnp.int32)
-    send_start = jnp.cumsum(send_row, dtype=jnp.int32) - send_row
-    slot_rows = jnp.minimum(send_start[:, None] + slots[None, :], frames - 1)
-    slot_used = slots[None, :] < send_row[:, None]
-    outgoing = targets[slot_rows]
-    out_mask = jnp.where(slot_used, valid[slot_rows], False).astype(jnp.bfloat16)
-    incoming, in_mask = (
-        lax.all_to_all(outgoing, "dp", split_axis=0, concat_axis=0, tiled=True),
-        lax.all_to_all(out_mask, "dp", split_axis=0, concat_axis=0, tiled=True),
+
+    def slot_rows(counts):
+        start = jnp.cumsum(counts, dtype=jnp.int32) - counts
+        rows = jnp.where(slots[None, :] < counts[:, None], start[:, None] + slots[None, :], -1)
+        return rows.reshape(-1)
+
+    pick = (slot_rows(recv_col)[:, None] == positions[None, :]).astype(jnp.bfloat16)
+    outgoing = jnp.dot(pick, student_in, preferred_element_type=jnp.float32).astype(jnp.bfloat16)
+    incoming = lax.all_to_all(
+        outgoing.reshape(owner_count, capacity, -1), "dp", split_axis=0, concat_axis=0, tiled=True
     )
-    recv_end = jnp.cumsum(recv_col, dtype=jnp.int32)
-    recv_start = recv_end - recv_col
-    source_of = jnp.sum(
-        (recv_end[None, :] <= positions[:, None]).astype(jnp.int32), axis=1, dtype=jnp.int32
+    place = (positions[:, None] == slot_rows(send_row)[None, :]).astype(jnp.bfloat16)
+    student = jnp.dot(
+        place, incoming.reshape(owner_count * capacity, -1), preferred_element_type=jnp.float32
+    ).astype(jnp.bfloat16)
+    target, (full_in, full_out, full_head) = teacher_targets(
+        (hid_whisper, hid_beats, hid_wavlm),
+        (up_whisper, up_beats, up_wavlm),
+        (down_whisper, down_beats, down_wavlm),
+        (w_in, w_out, w_head),
     )
-    select = jnp.arange(owner_count, dtype=jnp.int32)[None, :] == source_of[:, None]
-    within = positions - jnp.sum(jnp.where(select, recv_start[None, :], 0), axis=1, dtype=jnp.int32)
-    flat_slot = source_of * capacity + within
-    target = incoming.reshape(owner_count * capacity, incoming.shape[2])[flat_slot]
-    frame_mask = in_mask.reshape(owner_count * capacity)[flat_slot].astype(jnp.float32)
-    full_in, full_out, full_head = (
-        lax.all_gather(w_in, "dp", axis=0, tiled=True),
-        lax.all_gather(w_out, "dp", axis=0, tiled=True),
-        lax.all_gather(w_head, "dp", axis=0, tiled=True),
-    )
-    pre_act = jnp.dot(student_in, full_in, preferred_element_type=jnp.float32)
+    pre_act = jnp.dot(student, full_in, preferred_element_type=jnp.float32)
     activated = swoosh_low(pre_act).astype(jnp.bfloat16)
     features = (
-        student_in.astype(jnp.float32)
+        student.astype(jnp.float32)
         + jnp.dot(activated, full_out, preferred_element_type=jnp.float32)
     ).astype(jnp.bfloat16)
     predicted = jnp.dot(features, full_head, preferred_element_type=jnp.float32)
@@ -279,7 +449,7 @@
     )
     act_grad = jnp.dot(feat_grad, full_out.T, preferred_element_type=jnp.float32)
     pre_grad = (act_grad * swoosh_slope(pre_act)).astype(jnp.bfloat16)
-    return reduce_grads(student_in, activated, features, pre_grad, feat_grad, err_grad)
+    return reduce_grads(student, activated, features, pre_grad, feat_grad, err_grad)
 
 
 def solution(mesh):

time: 300 us -> 140 us (0.47)
  waiting for transfers between devices: 110 us -> 0.01 us
  Pallas kernels: 46.4 us -> 116 us
  matrix products: 40.4 us -> 6.81 us
  other arithmetic: 24.3 us -> 1.26 us
  local copies, waits for them, and re-layouts: 28.4 us -> 5.94 us
  blocking collectives: 17.4 us -> 0 us
  between operations: 16.3 us -> 1.54 us
  starting transfers between devices: 15.3 us -> 8.25 us
    pallas_call x0 -> x1, Pallas kernels: none -> 71.5 us  [teacher_targets(): pl.pallas_call(teacher_kernel, out_shape=[jax.ShapeDtypeStruct((128, 3072...]
    all_gather x5 -> x0, waiting for transfers between devices: 65.1 us -> none  [the longest x1 37.4 us: body(): lax.all_gather(w_head, 'dp', axis=0, tiled=True)]
    reduce_scatter x1 -> x0, waiting for transfers between devices: 43.2 us -> none  [body(): lax.psum_scatter(jnp.concatenate(pieces, axis=1), 'teacher', scatter_dime...]
    dot_general x4 -> x3, matrix products: 33.3 us -> 3.46 us  [the longest x1 2.28 us: body(): pre_act = jnp.dot(student, full_in, preferred_element_type=jnp.float32)]
    all_gather x1 -> x0, blocking collectives: 17.4 us -> none  [body(): lax.all_gather(normed_beats, 'teacher', axis=0, tiled=True)]
    gather x6 -> x0, local copies, waits for them, and re-layouts: 13.2 us -> none  [the longest x1 5.55 us: body(): outgoing = targets[slot_rows]]
    convert_element_type x6 -> x1, other arithmetic: 7.08 us -> 0.01 us  [body(): frame_mask = (positions % clip_slots < lengths).astype(jnp.float32)]
    all_to_all x2 -> x1, starting transfers between devices: 15.1 us -> 8.25 us  [body(): lax.all_to_all(outgoing.reshape(owner_count, capacity, -1), 'dp', split_a...]
  transfers between devices with their start and end apart: 8 -> 1, of which waited for: 4 -> 0; matrix products, arithmetic and copies ran while one was open for 21% -> 1% of each run, Pallas kernels for 0% -> 51%
where the time goes in v2:
time: 140 us
  Pallas kernels  116 us (83%)
  starting transfers between devices  8.25 us (6%)
  matrix products  6.81 us (5%)
  local copies, waits for them, and re-layouts  5.94 us (4%)
  between operations  1.54 us (1%)
    pallas_call x1, Pallas kernels, teacher_targets(): pl.pallas_call(teacher_kernel, out_shape=[jax.ShapeDtypeStruct((128, 3072...  71.5 us
    pallas_call x1, Pallas kernels, reduce_grads(): pl.pallas_call(grad_kernel, out_shape=jax.ShapeDtypeStruct((4, 48, 512),...  44.5 us
    all_to_all x1, starting transfers between devices, body(): lax.all_to_all(outgoing.reshape(owner_count, capacity, -1), 'dp', split_a...  8.25 us
  transfers between devices with their start and end apart: 1, of which 0 were waited for; matrix products, arithmetic and copies ran while one was open for 1% of the time, Pallas kernels for 51%

profile of v2, /device:TPU:0, one launch (start us, length us, event | category | flops | bytes accessed | tf_op | source)
XLA Modules:
  0.0 139.8 jit_solution(6009191840972047340)
XLA Ops:
  0.6 0.9 dynamic-slice_reduce_fusion
  1.6 0.1 reduce.6
  1.8 0.1 select_n.60
  2.0 1.0 fusion.4
  2.9 8.2 %all-to-all-start = ((bf16[32,8,512]{2,1,0:T(8,128)(2,1)}), bf16[32,8,512]{2,1,0:T(8,128)(2,1)S(1)}, u32[]{:S(2)}, u32[]{:S(2)}) async-start(bf16[32,8,512]{2,1,0:T(8,128)(2,1)} %fusion.4), calls=%async_computation | async-start | bytes 524288 | tf_op jit(solution)/shard_map/all_to_all | solution.py:424
  11.2 0.7 fusion.25
  12.0 0.1 reduce.4
  12.2 0.7 fusion.31
  13.7 71.5 %shard_map.169 = (bf16[128,3072]{1,0:T(8,128)(2,1)}, bf16[4,4,2,16,1536]{4,3,2,1,0:T(8,128)(2,1)}, bf16[4,4,2,48,512]{4,3,2,1,0:T(8,128)(2,1)}, bf16[4,4,2,16,3072]{4,3,2,1,0:T(8,128)(2,1)}) custom-call(bf16[128,1280]{1,0:T(8,128)(2,1)} %refs_0_.1, bf16[128,768]{1,0:T(8,128)(2,1)} %refs_1_.1, bf16[128,1024]{1,0:T(8,128)(2,1)} %refs_2_.1, ...), custom_call_target="tpu_custom_call" | custom-call | tf_op jit(solution)/shard_map/pallas_call | solution.py:368
  85.2 0.2 convolution_convert_fusion.1
  85.4 2.3 %fusion.7 = (bf16[1536,128]{0,1:T(8,128)(2,1)S(1)}, f32[128,1536]{1,0:T(8,128)S(1)}) fusion(bf16[128,512]{1,0:T(8,128)(2,1)S(1)} %convolution_convert_fusion.1, bf16[512,1536]{1,0:T(8,128)(2,1)} %bitcast.114), kind=kOutput, calls=%fused_computation.14 | convolution fusion | flops 203489280 | bytes 2883584 | tf_op jit(solution)/shard_map/dot_general | solution.py:437
  87.7 0.7 fusion.21
  88.4 1.2 copy-done.1
  89.6 0.2 copy-done.2
  89.8 0.8 fusion.2.err
  90.6 1.2 convolution_convert_fusion.2.fgrad
  91.8 0.7 fusion.3.pre
  92.5 0.2 copy.31
  92.8 0.1 copy.34
  92.9 0.1 copy.28
  93.1 44.5 %shard_map.170 = f32[4,48,512]{2,1,0:T(8,128)S(1)} custom-call(bf16[2,4,4,16,128]{4,3,2,1,0:T(8,128)(2,1)S(1)} %get-tuple-element.51.in_t, bf16[2,4,4,48,128]{4,3,2,1,0:T(8,128)(2,1)S(1)} %pad_maximum_fusion.act_t, bf16[2,4,4,16,128]{4,3,2,1,0:T(8,128)(2,1)S(1)} %get-tuple-element.52.feat_t, bf16[128,1536]{1,0:T(8,128)(2,1)S(1)} %fusion.3.pre, ...), custom_call_target="tpu_custom_call" | custom-call | tf_op jit(solution)/shard_map/pallas_call | solution.py:173
  137.7 0.7 slice_bitcast_fusion.1
  138.4 0.7 copy.45
  139.1 0.7 copy.46
  (27 shorter events, 0.7 us)
Async XLA Ops:
  0.6 1.3 copy-start
  2.9 82.2 %all-to-all-start = ((bf16[32,8,512]{2,1,0:T(8,128)(2,1)}), bf16[32,8,512]{2,1,0:T(8,128)(2,1)S(1)}, u32[]{:S(2)}, u32[]{:S(2)}) async-start(bf16[32,8,512]{2,1,0:T(8,128)(2,1)} %fusion.4), calls=%async_computation | async-start | bytes 524288 | tf_op jit(solution)/shard_map/all_to_all | solution.py:424
  85.4 2.3 %copy-start.4 = (bf16[4,4,2,48,512]{4,3,2,1,0:T(8,128)(2,1)S(1)}, bf16[4,4,2,48,512]{4,3,2,1,0:T(8,128)(2,1)}, u32[]{:S(2)}) copy-start(bf16[4,4,2,48,512]{4,3,2,1,0:T(8,128)(2,1)} %get-tuple-element.32) | copy-start | bytes 4718596
  87.7 1.9 %copy-start.1 = (bf16[4,4,2,16,3072]{4,3,2,1,0:T(8,128)(2,1)S(1)}, bf16[4,4,2,16,3072]{4,3,2,1,0:T(8,128)(2,1)}, u32[]{:S(2)}) copy-start(bf16[4,4,2,16,3072]{4,3,2,1,0:T(8,128)(2,1)} %get-tuple-element.33) | copy-start | bytes 9437188
  87.7 2.1 %copy-start.2 = (bf16[128,3072]{1,0:T(8,128)(2,1)S(1)}, bf16[128,3072]{1,0:T(8,128)(2,1)}, u32[]{:S(2)}) copy-start(bf16[128,3072]{1,0:T(8,128)(2,1)} %get-tuple-element.34) | copy-start | bytes 2359300
  87.7 2.1 %copy-start.3 = (f32[3072]{0:T(1024)S(1)}, f32[3072]{0:T(1024)}, u32[]{:S(2)}) copy-start(f32[3072]{0:T(1024)} %constant.138.clone.1) | copy-start | bytes 36868

commit v3 on v0

v3 whole, which is shorter than its diff:
```python
import functools

import jax
import jax.numpy as jnp
from jax import lax
from jax.experimental import pallas as pl
from jax.experimental.pallas import tpu as pltpu
from jax.sharding import PartitionSpec as P

WH = 1280
WB = 768
WL = 1024
EPS = 1e-05


def layer_norm(values):
    wide = values.astype(jnp.float32)
    center = wide - jnp.mean(wide, axis=-1, keepdims=True)
    spread = jnp.mean(center * center, axis=-1, keepdims=True)
    return center * lax.rsqrt(spread + EPS)


MESH_ID = pl.DeviceIdType.MESH
TEACHERS = ((2, WL, WH + WB), (0, WH, 0), (1, WB, WH))
SPAN = 6144
GROUP_COLUMNS = ((0, 1024), (1024, 1280), (2304, 3840))


def gelu(values):
    return 0.5 * values * (1.0 + lax.erf(values * 0.7071067811865476))


def dot(a, b):
    return jnp.dot(a, b, preferred_element_type=jnp.float32)


def dot_t(a, b):
    return lax.dot_general(a, b, (((1,), (1,)), ((), ())), preferred_element_type=jnp.float32)


def scratch_plan():
    bf, f32 = jnp.bfloat16, jnp.float32
    vm, dma = pltpu.VMEM, pltpu.SemaphoreType.DMA
    plan = {}
    for k, w in enumerate((WH, WB, WL)):
        plan[f"vup{k}"] = vm((w, w), bf)
        plan[f"vdown{k}"] = vm((w, w), bf)
        plan[f"normed{k}"] = vm((4, 128, w), bf)
        plan[f"keep{k}"] = vm((128, w), f32)
        plan[f"part{k}"] = vm((2, 128, w), f32)
        plan[f"sopp{k}"] = vm((2, 64, w), bf)
        plan[f"ropp{k}"] = vm((2, 64, w), bf)
        plan[f"sside{k}"] = vm((2, 128, w), bf)
        plan[f"rside{k}"] = vm((2, 128, w), bf)
    for m, (h, w) in enumerate(((16, 1536), (48, 512), (16, 3072))):
        plan[f"full{m}"] = vm((4, 4, 2, h, w), bf)
    plan.update(
        hidden=vm((256, WH), bf),
        outgoing=vm((32, 8, 512), HAND), incoming=vm((32, 8, 512), HAND),
        student=vm((128, 512), bf),
        slope=vm((128, 1536), f32), predicted=vm((128, 3072), f32), fgrad=vm((128, 512), f32),
        tin=vm((4, 4, 2, 16, 128), bf), tact=vm((4, 4, 2, 48, 128), bf), tfeat=vm((4, 4, 2, 16, 128), bf),
        lin=vm((4, 4, 16, 256), bf), lact=vm((4, 4, 48, 256), bf), lfeat=vm((4, 4, 16, 256), bf),
        rpre=vm((256, 1536), bf), rfg=vm((256, 512), bf), rerr=vm((256, 3072), bf),
        own1=vm((4, 16, SPAN), f32), send1=vm((3, 4, 16, SPAN), bf), recv1=vm((3, 4, 16, SPAN), bf),
        own2=vm((16, SPAN), f32), send2=vm((3, 16, SPAN), bf), recv2=vm((3, 16, SPAN), bf),
        send3=vm((4, 16, 1536), bf), recv3=vm((3, 16, 1536), bf), mine3=vm((16, 1536), f32),
        wsem=dma((6,)),
        ags=dma((3, 2)), agr=dma((3, 2)), fws=dma((3, 2)), fwr=dma((3, 2)),
        ops=dma((3, 2)), opr=dma((3, 2)), sds=dma((3, 2)), sdr=dma((3, 2)),
        w1s=dma((3, 3)), w1r=dma((3, 3)), w2s=dma((3, 3, 4)), w2r=dma((3, 3, 4)), w3s=dma((3,)), w3r=dma((3,)),
        hos=dma((32,)), hor=dma((32,)),
        xs=dma((8,)), xr=dma((8,)),
        s1s=dma((3, 3)), s1r=dma((3, 3)), s2s=dma((3, 3)), s2r=dma((3, 3)),
        s3s=dma((3,)), s3r=dma((3,)), s4s=dma((3,)), s4r=dma((3,)),
    )
    return plan


HAND = jnp.bfloat16


def step_kernel(names, *refs):
    hid = refs[0:3]
    ups, downs = refs[3:9:2], refs[4:9:2]
    shards = refs[9:12]
    student_in, counts_ref, clip_ref, out = refs[12:16]
    r = dict(zip(names, refs[16:]))
    per = lambda name: [r[f"{name}{k}"] for k in range(3)]
    vup, vdown, normed, keep, part = per("vup"), per("vdown"), per("normed"), per("keep"), per("part")
    sopp, ropp, sside, rside, full = per("sopp"), per("ropp"), per("sside"), per("rside"), per("full")
    hidden, rerr, rfg, rpre = r["hidden"], r["rerr"], r["rfg"], r["rpre"]
    bf, f32 = jnp.bfloat16, jnp.float32

    y = lax.axis_index("teacher")
    dp = lax.axis_index("dp")
    c = dp % 2
    z = (dp // 2) % 4
    x = dp // 8
    swap = c == 1
    first = jnp.where(swap, z, x)
    second = jnp.where(swap, x, z)
    at_y = lambda t: {"teacher": t % 4}
    right, left = at_y(y + 1), at_y(y + 3)
    pair = {"dp": (x * 4 + z) * 2 + (1 - c)}

    def at_first(a):
        return {"dp": jnp.where(swap, (x * 4 + a) * 2 + 1, (a * 4 + z) * 2)}

    def at_second(b):
        return {"dp": jnp.where(swap, (b * 4 + z) * 2 + 1, (x * 4 + b) * 2)}

    def send(src, dst, ssem, rsem, dev):
        cp = pltpu.make_async_remote_copy(
            src_ref=src, dst_ref=dst, send_sem=ssem, recv_sem=rsem,
            device_id=dev, device_id_type=MESH_ID)
        cp.start()
        return cp

    def finish_all(copies):
        for cp in copies:
            cp.wait()

    loads = {}
    for n, (k, _, _) in enumerate(TEACHERS):
        loads[k] = (pltpu.make_async_copy(ups[k], vup[k], r["wsem"].at[2 * n]),
                    pltpu.make_async_copy(downs[k], vdown[k], r["wsem"].at[2 * n + 1]))
        for cp in loads[k]:
            cp.start()

    barrier = pltpu.get_barrier_semaphore()
    for d in range(1, 4):
        pl.semaphore_signal(barrier, inc=1, device_id=at_y(y + d), device_id_type=MESH_ID)
    for d in range(1, 32):
        pl.semaphore_signal(barrier, inc=1, device_id={"dp": (dp + d) % 32}, device_id_type=MESH_ID)
    order = [k for k, _, _ in TEACHERS]
    normed[order[0]][0] = layer_norm(hid[order[0]][...]).astype(bf)

    counts = counts_ref[...].astype(f32)
    iota = lambda shape, axis: lax.broadcasted_iota(jnp.int32, shape, axis)
    src_at, own_at = iota((32, 32), 0), iota((32, 32), 1)
    one = lambda hit: jnp.where(hit, 1.0, 0.0)
    exact = lambda v: v.astype(bf)
    before_src = dot(exact(one(own_at < src_at)), exact(counts))
    before_own = dot(exact(counts), exact(one(src_at < own_at)))
    my_col, my_row = one(own_at == dp), one(src_at == dp)
    row_at, slot_at = iota((256, 32), 0), iota((256, 32), 1) * 8
    spread = exact(one((row_at >= slot_at) & (row_at < slot_at + 8)))
    wide_col = lambda v: dot(spread, exact(jnp.broadcast_to(jnp.sum(v * my_col, axis=1, keepdims=True), (32, 128))))
    slot = (iota((256, 128), 0) & 7).astype(f32)
    hit = (iota((256, 128), 1).astype(f32) == wide_col(before_src) + slot) & (slot < wide_col(counts))
    leaving = dot(exact(one(hit)), student_in[...])
    r["outgoing"][...] = leaving.reshape(32, 8, 512).astype(HAND)
    r["incoming"][dp] = r["outgoing"][dp]
    slot_at2, col_at = iota((32, 256), 0) * 8, iota((32, 256), 1)
    spread2 = exact(one((col_at >= slot_at2) & (col_at < slot_at2 + 8)))
    wide_row = lambda v: dot(exact(jnp.broadcast_to(jnp.sum(v * my_row, axis=0, keepdims=True), (128, 32))), spread2)
    slot2 = (iota((128, 256), 1) & 7).astype(f32)
    hit2 = (iota((128, 256), 0).astype(f32) == wide_row(before_own) + slot2) & (slot2 < wide_row(counts))
    place = exact(one(hit2))
    mask = one(iota((128, 1), 0) < clip_ref[0])

    for m in range(3):
        full[m][x, z, c] = shards[m][...]
    pl.semaphore_wait(barrier, 34)

    def gather_out(k):
        return (send(normed[k].at[0], normed[k].at[1], r["ags"].at[k, 0], r["agr"].at[k, 0], right),
                send(normed[k].at[0], normed[k].at[2], r["ags"].at[k, 1], r["agr"].at[k, 1], left))

    def forward(k):
        lo, hi = pl.ds(0, 64), pl.ds(64, 64)
        return (send(normed[k].at[1, lo], normed[k].at[3, lo], r["fws"].at[k, 0], r["fwr"].at[k, 0], right),
                send(normed[k].at[2, hi], normed[k].at[3, hi], r["fws"].at[k, 1], r["fwr"].at[k, 1], left))

    def ffn(k, width, at, count, store):
        rows = count * 128
        values = normed[k][at:at + count].reshape(rows, width)
        for j in range(width // 256):
            cols = slice(256 * j, 256 * j + 256)
            hidden[0:rows, cols] = gelu(dot(values, vup[k][:, cols])).astype(bf)
        for j in range(width // 256):
            cols = slice(256 * j, 256 * j + 256)
            store(cols, dot(hidden[0:rows, 0:width], vdown[k][:, cols]))

    gathers = {order[0]: gather_out(order[0])}
    hand = []
    for d in range(1, 32):
        to = (dp + d) % 32
        hand.append(send(r["outgoing"].at[to], r["incoming"].at[dp], r["hos"].at[d], r["hor"].at[d], {"dp": to}))
    stage1 = []
    for d in (2, 1, 3):
        for m in range(3):
            stage1.append(send(shards[m], full[m].at[x, z, c], r["w1s"].at[d - 1, m], r["w1r"].at[d - 1, m],
                               at_first((first + d) % 4)))
    for k in order[1:]:
        normed[k][0] = layer_norm(hid[k][...]).astype(bf)
    gathers[order[1]] = gather_out(order[1])
    stage2, stage3 = [], []

    def weights_second():
        finish_all(stage1)
        for d in (2, 1, 3):
            dev = at_second((second + d) % 4)
            for m in range(3):
                for i in range(4):
                    place_at = full[m].at[jnp.where(swap, x, i), jnp.where(swap, i, z), c]
                    stage2.append(send(place_at, place_at, r["w2s"].at[d - 1, m, i], r["w2r"].at[d - 1, m, i], dev))

    def weights_third():
        finish_all(stage2)
        for m in range(3):
            half = full[m].at[:, :, c]
            stage3.append(send(half, half, r["w3s"].at[m], r["w3r"].at[m], pair))

    opposite, sides = {}, {}

    def send_sides(k):
        finish_all(opposite[k])
        sside[k][0, 0:64] = part[k][0, 0:64].astype(bf)
        sside[k][0, 64:128] = (part[k][0, 64:128] + ropp[k][1].astype(f32)).astype(bf)
        sside[k][1, 0:64] = (part[k][1, 0:64] + ropp[k][0].astype(f32)).astype(bf)
        sside[k][1, 64:128] = part[k][1, 64:128].astype(bf)
        sides[k] = (send(sside[k].at[1], rside[k].at[0], r["sds"].at[k, 0], r["sdr"].at[k, 0], right),
                    send(sside[k].at[0], rside[k].at[1], r["sds"].at[k, 1], r["sdr"].at[k, 1], left))

    def pair_send(i, src, dst):
        return send(src, dst, r["xs"].at[i], r["xr"].at[i], pair)

    def share_rows(i, values, h, mine, joined):
        mine[...] = values.T.reshape(4, 4, 2, h, 128)
        joined[:, :, :, 0:128] = mine[:, :, c]
        return pair_send(i, mine.at[:, :, 1 - c], joined.at[:, :, :, pl.ds(128, 128)])

    shared = {}
    for n, (k, width, _) in enumerate(TEACHERS):
        finish_all(loads[k])

        def put_keep(cols, v):
            keep[k][:, cols] = v
        ffn(k, width, 0, 1, put_keep)
        finish_all(gathers[k])
        passed = forward(k)
        if n == 0:
            gathers[order[2]] = gather_out(order[2])
        if n == 1:
            send_sides(order[0])

        def put_part(cols, v):
            part[k][:, :, cols] = v.reshape(2, 128, 256)
        ffn(k, width, 1, 2, put_part)
        if n == 0:
            weights_second()
            finish_all(hand)
            student = dot(place, r["incoming"][...].reshape(256, 512).astype(bf)).astype(bf)
            r["student"][...] = student
            shared["in"] = share_rows(0, student, 16, r["tin"], r["lin"])
        if n == 1:
            weights_third()
        finish_all(passed)

        def put_opp(cols, v):
            sopp[k][:, :, cols] = v.astype(bf).reshape(2, 64, 256)
        ffn(k, width, 3, 1, put_opp)
        opposite[k] = (send(sopp[k].at[0], ropp[k].at[0], r["ops"].at[k, 0], r["opr"].at[k, 0], right),
                       send(sopp[k].at[1], ropp[k].at[1], r["ops"].at[k, 1], r["opr"].at[k, 1], left))
    send_sides(order[1])
    finish_all(stage3)
    student = r["student"][...]
    pre_act = dot(student, full[0][...].reshape(512, 1536))
    shifted = pre_act - 4.0
    soft = jnp.maximum(shifted, 0.0) + jnp.log1p(jnp.exp(-jnp.abs(shifted)))
    activated = (soft - 0.08 * pre_act - 0.035).astype(bf)
    r["slope"][...] = jax.nn.sigmoid(shifted) - 0.08
    features = (student.astype(f32) + dot(activated, full[1][...].reshape(1536, 512))).astype(bf)
    send_sides(order[2])
    shared["feat"] = share_rows(1, features, 16, r["tfeat"], r["lfeat"])
    shared["act"] = share_rows(2, activated, 48, r["tact"], r["lact"])
    for k, width, start in TEACHERS:
        r["predicted"][:, start:start + width] = dot(features, full[2][:, :, :, :, start:start + width].reshape(512, width))

    def error_of(n):
        k, width, start = TEACHERS[n]
        cols = slice(start, start + width)
        finish_all(sides[k])
        total = hid[k][...].astype(f32) + keep[k][...] + rside[k][0].astype(f32) + rside[k][1].astype(f32)
        target = total.astype(bf).astype(f32)
        err = ((r["predicted"][:, cols] - target) * (2.0 / width) * mask).astype(bf)
        rerr[0:128, cols] = err
        cp = pair_send(3 + n, rerr.at[pl.ds(0, 128), pl.ds(start, width)], rerr.at[pl.ds(128, 128), pl.ds(start, width)])
        back = dot_t(err, full[2][:, :, :, :, cols].reshape(512, width))
        if n == 0:
            r["fgrad"][...] = back
        elif n == 1:
            r["fgrad"][...] += back
        else:
            back = r["fgrad"][...] + back
        return cp, back

    def block_rows(joined, a):
        tiles = [joined[jnp.where(swap, b, a), jnp.where(swap, a, b)] for b in range(4)]
        return jnp.concatenate(tiles, axis=0)

    def products(n, a, store):
        heads = block_rows(r["lfeat"], a)
        if n < 2:
            _, width, start = TEACHERS[n]
            store(GROUP_COLUMNS[n][0], dot(heads, rerr[:, start:start + width]).reshape(4, 16, width))
        else:
            store(2304, dot(block_rows(r["lin"], a), rpre[...]).reshape(4, 16, 1536))
            store(3840, dot(heads, rerr[:, WH:WH + WB]).reshape(4, 16, WB))
            outs = dot(block_rows(r["lact"], a), rfg[...]).reshape(4, 48, 512)
            for m in range(3):
                store(4608 + 512 * m, outs[:, 16 * m:16 * m + 16])

    phase1, phase2 = {}, {}

    def start_group(n):
        start, width = GROUP_COLUMNS[n]
        cols = pl.ds(start, width)
        copies = []
        for d in (2, 1, 3):
            a = (first + d) % 4

            def put(at, v):
                r["send1"][d - 1, :, :, at:at + v.shape[2]] = v.astype(bf)
            products(n, a, put)
            copies.append(send(r["send1"].at[d - 1, :, :, cols], r["recv1"].at[d - 1, :, :, cols],
                               r["s1s"].at[n, d - 1], r["s1r"].at[n, d - 1], at_first(a)))

        def put_own(at, v):
            r["own1"][:, :, at:at + v.shape[2]] = v
        products(n, first, put_own)
        phase1[n] = copies

    def next_group(n):
        start, width = GROUP_COLUMNS[n]
        cols = slice(start, start + width)
        ref_cols = pl.ds(start, width)
        finish_all(phase1[n])

        def total1(b):
            v = r["own1"][b, :, cols]
            for i in range(3):
                v = v + r["recv1"][i, b, :, cols].astype(f32)
            return v
        copies = []
        for d in (2, 1, 3):
            b = (second + d) % 4
            r["send2"][d - 1, :, cols] = total1(b).astype(bf)
            copies.append(send(r["send2"].at[d - 1, :, ref_cols], r["recv2"].at[d - 1, :, ref_cols],
                               r["s2s"].at[n, d - 1], r["s2r"].at[n, d - 1], at_second(b)))
        r["own2"][:, cols] = total1(second)
        phase2[n] = copies

    cp, _ = error_of(0)
    finish_all([cp, shared["feat"]])
    start_group(0)
    cp, _ = error_of(1)
    cp.wait()
    start_group(1)
    finish_all([shared["in"], shared["act"]])
    next_group(0)
    cp, back = error_of(2)
    feat_grad = back.astype(bf)
    rfg[0:128] = feat_grad
    late = [cp, pair_send(6, rfg.at[pl.ds(0, 128)], rfg.at[pl.ds(128, 128)])]
    act_grad = dot_t(feat_grad, full[1][...].reshape(1536, 512))
    rpre[0:128] = (act_grad * r["slope"][...]).astype(bf)
    late.append(pair_send(7, rpre.at[pl.ds(0, 128)], rpre.at[pl.ds(128, 128)]))
    finish_all(late)
    start_group(2)
    next_group(1)
    next_group(2)
    for n in range(3):
        finish_all(phase2[n])
    total = r["own2"][...]
    for i in range(3):
        total = total + r["recv2"][i].astype(f32)
    r["own2"][...] = total
    for t in range(4):
        r["send3"][t] = total[:, 1536 * t:1536 * t + 1536].astype(bf)
    copies = []
    for d in (2, 1, 3):
        t = (y + d) % 4
        copies.append(send(r["send3"].at[t], r["recv3"].at[d - 1], r["s3s"].at[d - 1], r["s3r"].at[d - 1], at_y(t)))
    finish_all(copies)
    final = r["own2"][:, pl.ds(pl.multiple_of(y * 1536, 1536), 1536)]
    for i in range(3):
        final = final + r["recv3"][i].astype(f32)
    r["mine3"][...] = final
    out[y] = final
    copies = []
    for d in (2, 1, 3):
        t = (y + d) % 4
        copies.append(send(r["mine3"], out.at[y], r["s4s"].at[d - 1], r["s4r"].at[d - 1], at_y(t)))
    finish_all(copies)


def body(
    hid_whisper, hid_beats, hid_wavlm,
    up_whisper, down_whisper, up_beats, down_beats, up_wavlm, down_wavlm,
    clip_len, send_counts, student_in, w_in, w_out, w_head,
):
    vm = pl.BlockSpec(memory_space=pltpu.VMEM)
    hbm = pl.BlockSpec(memory_space=pl.ANY)
    plan = scratch_plan()
    out = pl.pallas_call(
        functools.partial(step_kernel, tuple(plan)),
        out_shape=jax.ShapeDtypeStruct((4, 16, 1536), jnp.float32),
        in_specs=[vm] * 3 + [hbm] * 6 + [vm] * 5 + [pl.BlockSpec(memory_space=pltpu.SMEM)],
        out_specs=vm,
        scratch_shapes=list(plan.values()),
        compiler_params=pltpu.CompilerParams(
            collective_id=0, has_side_effects=True, vmem_limit_bytes=60 * 1024 * 1024),
    )(
        hid_whisper, hid_beats, hid_wavlm,
        up_whisper, down_whisper, up_beats, down_beats, up_wavlm, down_wavlm,
        w_in, w_out, w_head, student_in, send_counts[0], clip_len,
    )
    flat = out.transpose(1, 0, 2).reshape(16, SPAN)
    grad_in = flat[:, 2304:3840]
    grad_out = flat[:, 4608:].reshape(16, 3, 512).transpose(1, 0, 2).reshape(48, 512)
    grad_head = jnp.concatenate([flat[:, 1024:2304], flat[:, 3840:4608], flat[:, 0:1024]], axis=1)
    return grad_in, grad_out, grad_head


def solution(mesh):
    in_specs = (
        P(("teacher", "dp"), None),
        P(("teacher", "dp"), None),
        P(("teacher", "dp"), None),
        P(None, "teacher"),
        P("teacher", None),
        P(None, "teacher"),
        P("teacher", None),
        P(None, "teacher"),
        P("teacher", None),
        P(("teacher", "dp")),
        P("teacher", None, None),
        P(("teacher", "dp"), None),
        P("dp", None),
        P("dp", None),
        P("dp", None),
    )
    out_specs = (P("dp", None), P("dp", None), P("dp", None))
    return jax.shard_map(body, mesh=mesh, in_specs=in_specs, out_specs=out_specs, check_vma=False)
```

time: 561 us -> 105 us (0.19)
  waiting for transfers between devices: 413 us -> 0 us
  Pallas kernels: 0 us -> 100 us
  matrix products: 52 us -> 0 us
  local copies, waits for them, and re-layouts: 26.8 us -> 2.44 us
  other arithmetic: 20 us -> 0.69 us
  blocking collectives: 17.4 us -> 0 us
  starting transfers between devices: 15.5 us -> 0 us
  between operations: 16.1 us -> 1.31 us
    reduce_scatter x3 -> x0, waiting for transfers between devices: 221 us -> none  [the longest x1 89.3 us: body(): lax.psum_scatter(head_term, 'dp', scatter_dimension=0, tiled=True)]
    pallas_call x0 -> x1, Pallas kernels: none -> 100 us  [body(): pl.pallas_call(functools.partial(step_kernel, tuple(plan)), out_shape=jax...]
    unnamed x11 -> x0, waiting for transfers between devices: 72.9 us -> none
    all_gather x5 -> x0, waiting for transfers between devices: 68.4 us -> none  [the longest x1 40.2 us: body(): lax.all_gather(w_head, 'dp', axis=0, tiled=True)]
    dot_general x10 -> x0, matrix products: 52 us -> none  [the longest x3 30.1 us: body(): jnp.dot(hidden, down_proj, preferred_element_type=jnp.float32)]
    psum x1 -> x0, waiting for transfers between devices: 45.5 us -> none  [body(): grads = lax.psum((shards[0], shards[1], shards[2]), 'teacher')]
    all_gather x1 -> x0, blocking collectives: 17.4 us -> none  [body(): lax.all_gather(normed_beats, 'teacher', axis=0, tiled=True)]
    all_to_all x2 -> x0, starting transfers between devices: 14.8 us -> none  [the longest x1 7.48 us: body(): lax.all_to_all(outgoing, 'dp', split_axis=0, concat_axis=0, tiled=True)]
  transfers between devices with their start and end apart: 12 -> 0, of which waited for: 9 -> 0; matrix products, arithmetic and copies ran while one was open for 10% -> 0% of each run, Pallas kernels for 0% -> 0%
where the time goes in v3:
time: 105 us
  Pallas kernels  100 us (95%)
  local copies, waits for them, and re-layouts  2.44 us (2%)
  between operations  1.31 us (1%)
    pallas_call x1, Pallas kernels, body(): pl.pallas_call(functools.partial(step_kernel, tuple(plan)), out_shape=jax...  100 us

profile of v3, /device:TPU:0, one launch (start us, length us, event | category | flops | bytes accessed | tf_op | source)
XLA Modules:
  0.0 104.5 jit_solution(3317210425018448282)
XLA Ops:
  1.3 100.1 %shard_map.166 = f32[4,16,1536]{2,1,0:T(8,128)} custom-call(bf16[128,1280]{1,0:T(8,128)(2,1)} %refs_0_.1, bf16[128,768]{1,0:T(8,128)(2,1)} %refs_1_.1, bf16[128,1024]{1,0:T(8,128)(2,1)} %refs_2_.1, bf16[1280,1280]{1,0:T(8,128)(2,1)} %refs_3_.1, bf16[1280,1280]{1,0:T(8,128)(2,1)} %refs_4_.1, bf16[768,768]{1,0:T(8,128)(2,1)} %refs_5_.1, ...), custom_call_target="tpu_custom_call" | custom-call | tf_op jit(solution)/shard_map/pallas_call | solution.py:408
  101.4 1.0 copy.22
  102.4 0.7 fusion
  103.0 0.1 reshape.16
  103.1 0.7 copy.21
  103.8 0.7 pad_maximum_fusion
  (3 shorter events, 0.0 us)

commit v4 on v3

--- a/solution.py
+++ b/solution.py
@@ -23,7 +23,8 @@
 MESH_ID = pl.DeviceIdType.MESH
 TEACHERS = ((2, WL, WH + WB), (0, WH, 0), (1, WB, WH))
 SPAN = 6144
-GROUP_COLUMNS = ((0, 1024), (1024, 1280), (2304, 3840))
+GROUP_COLUMNS = ((0, 1024), (1024, 1280), (2304, 2304), (4608, 1536))
+SUM_COLUMNS = ((0, 1024), (1024, 3584), (4608, 1536))
 
 
 def gelu(values):
@@ -43,6 +44,7 @@
     vm, dma = pltpu.VMEM, pltpu.SemaphoreType.DMA
     plan = {}
     for k, w in enumerate((WH, WB, WL)):
+        plan[f"hid{k}"] = vm((128, w), bf)
         plan[f"vup{k}"] = vm((w, w), bf)
         plan[f"vdown{k}"] = vm((w, w), bf)
         plan[f"normed{k}"] = vm((4, 128, w), bf)
@@ -64,15 +66,15 @@
         rpre=vm((256, 1536), bf), rfg=vm((256, 512), bf), rerr=vm((256, 3072), bf),
         own1=vm((4, 16, SPAN), f32), send1=vm((3, 4, 16, SPAN), bf), recv1=vm((3, 4, 16, SPAN), bf),
         own2=vm((16, SPAN), f32), send2=vm((3, 16, SPAN), bf), recv2=vm((3, 16, SPAN), bf),
-        send3=vm((4, 16, 1536), bf), recv3=vm((3, 16, 1536), bf), mine3=vm((16, 1536), f32),
-        wsem=dma((6,)),
+        sums=vm((4, 16, SPAN), bf),
+        rows_in=vm((128, 512), bf), counts=vm((32, 32), jnp.int32),
+        wsem=dma((6,)), isem=dma((8,)),
         ags=dma((3, 2)), agr=dma((3, 2)), fws=dma((3, 2)), fwr=dma((3, 2)),
         ops=dma((3, 2)), opr=dma((3, 2)), sds=dma((3, 2)), sdr=dma((3, 2)),
         w1s=dma((3, 3)), w1r=dma((3, 3)), w2s=dma((3, 3, 4)), w2r=dma((3, 3, 4)), w3s=dma((3,)), w3r=dma((3,)),
         hos=dma((32,)), hor=dma((32,)),
         xs=dma((8,)), xr=dma((8,)),
-        s1s=dma((3, 3)), s1r=dma((3, 3)), s2s=dma((3, 3)), s2r=dma((3, 3)),
-        s3s=dma((3,)), s3r=dma((3,)), s4s=dma((3,)), s4r=dma((3,)),
+        s1s=dma((4, 3)), s1r=dma((4, 3)), s2s=dma((4, 3)), s2r=dma((4, 3)), s3s=dma((3, 3)), s3r=dma((3, 3)),
     )
     return plan
 
@@ -81,17 +83,18 @@
 
 
 def step_kernel(names, *refs):
-    hid = refs[0:3]
     ups, downs = refs[3:9:2], refs[4:9:2]
     shards = refs[9:12]
-    student_in, counts_ref, clip_ref, out = refs[12:16]
-    r = dict(zip(names, refs[16:]))
+    clip_ref, grad_in, grad_out, grad_head = refs[14:18]
+    r = dict(zip(names, refs[18:]))
     per = lambda name: [r[f"{name}{k}"] for k in range(3)]
+    hid = per("hid")
     vup, vdown, normed, keep, part = per("vup"), per("vdown"), per("normed"), per("keep"), per("part")
     sopp, ropp, sside, rside, full = per("sopp"), per("ropp"), per("sside"), per("rside"), per("full")
     hidden, rerr, rfg, rpre = r["hidden"], r["rerr"], r["rfg"], r["rpre"]
     bf, f32 = jnp.bfloat16, jnp.float32
 
+    order = [k for k, _, _ in TEACHERS]
     y = lax.axis_index("teacher")
     dp = lax.axis_index("dp")
     c = dp % 2
@@ -121,6 +124,19 @@
         for cp in copies:
             cp.wait()
 
+    ready = {}
+    for i, (name, src, dst) in enumerate((
+        (order[0], refs[order[0]], hid[order[0]]),
+        ("counts", refs[13], r["counts"]),
+        ("rows", refs[12], r["rows_in"]),
+        ("in", shards[0], full[0].at[x, z, c]),
+        ("out", shards[1], full[1].at[x, z, c]),
+        ("head", shards[2], full[2].at[x, z, c]),
+        (order[1], refs[order[1]], hid[order[1]]),
+        (order[2], refs[order[2]], hid[order[2]]),
+    )):
+        ready[name] = pltpu.make_async_copy(src, dst, r["isem"].at[i])
+        ready[name].start()
     loads = {}
     for n, (k, _, _) in enumerate(TEACHERS):
         loads[k] = (pltpu.make_async_copy(ups[k], vup[k], r["wsem"].at[2 * n]),
@@ -133,10 +149,11 @@
         pl.semaphore_signal(barrier, inc=1, device_id=at_y(y + d), device_id_type=MESH_ID)
     for d in range(1, 32):
         pl.semaphore_signal(barrier, inc=1, device_id={"dp": (dp + d) % 32}, device_id_type=MESH_ID)
-    order = [k for k, _, _ in TEACHERS]
+    ready[order[0]].wait()
     normed[order[0]][0] = layer_norm(hid[order[0]][...]).astype(bf)
 
-    counts = counts_ref[...].astype(f32)
+    ready["counts"].wait()
+    counts = r["counts"][...].astype(f32)
     iota = lambda shape, axis: lax.broadcasted_iota(jnp.int32, shape, axis)
     src_at, own_at = iota((32, 32), 0), iota((32, 32), 1)
     one = lambda hit: jnp.where(hit, 1.0, 0.0)
@@ -149,7 +166,8 @@
     wide_col = lambda v: dot(spread, exact(jnp.broadcast_to(jnp.sum(v * my_col, axis=1, keepdims=True), (32, 128))))
     slot = (iota((256, 128), 0) & 7).astype(f32)
     hit = (iota((256, 128), 1).astype(f32) == wide_col(before_src) + slot) & (slot < wide_col(counts))
-    leaving = dot(exact(one(hit)), student_in[...])
+    ready["rows"].wait()
+    leaving = dot(exact(one(hit)), r["rows_in"][...])
     r["outgoing"][...] = leaving.reshape(32, 8, 512).astype(HAND)
     r["incoming"][dp] = r["outgoing"][dp]
     slot_at2, col_at = iota((32, 256), 0) * 8, iota((32, 256), 1)
@@ -160,8 +178,7 @@
     place = exact(one(hit2))
     mask = one(iota((128, 1), 0) < clip_ref[0])
 
-    for m in range(3):
-        full[m][x, z, c] = shards[m][...]
+    finish_all([ready["in"], ready["out"], ready["head"]])
     pl.semaphore_wait(barrier, 34)
 
     def gather_out(k):
@@ -191,9 +208,10 @@
     stage1 = []
     for d in (2, 1, 3):
         for m in range(3):
-            stage1.append(send(shards[m], full[m].at[x, z, c], r["w1s"].at[d - 1, m], r["w1r"].at[d - 1, m],
+            stage1.append(send(full[m].at[x, z, c], full[m].at[x, z, c], r["w1s"].at[d - 1, m], r["w1r"].at[d - 1, m],
                                at_first((first + d) % 4)))
     for k in order[1:]:
+        ready[k].wait()
         normed[k][0] = layer_norm(hid[k][...]).astype(bf)
     gathers[order[1]] = gather_out(order[1])
     stage2, stage3 = [], []
@@ -232,39 +250,59 @@
         joined[:, :, :, 0:128] = mine[:, :, c]
         return pair_send(i, mine.at[:, :, 1 - c], joined.at[:, :, :, pl.ds(128, 128)])
 
-    shared = {}
-    for n, (k, width, _) in enumerate(TEACHERS):
+    shared, passed = {}, {}
+    widths = [width for _, width, _ in TEACHERS]
+
+    def own_rows(n):
+        k = order[n]
         finish_all(loads[k])
 
-        def put_keep(cols, v):
+        def put(cols, v):
             keep[k][:, cols] = v
-        ffn(k, width, 0, 1, put_keep)
-        finish_all(gathers[k])
-        passed = forward(k)
-        if n == 0:
-            gathers[order[2]] = gather_out(order[2])
-        if n == 1:
-            send_sides(order[0])
-
-        def put_part(cols, v):
+        ffn(k, widths[n], 0, 1, put)
+
+    def side_rows(n):
+        k = order[n]
+
+        def put(cols, v):
             part[k][:, :, cols] = v.reshape(2, 128, 256)
-        ffn(k, width, 1, 2, put_part)
-        if n == 0:
-            weights_second()
-            finish_all(hand)
-            student = dot(place, r["incoming"][...].reshape(256, 512).astype(bf)).astype(bf)
-            r["student"][...] = student
-            shared["in"] = share_rows(0, student, 16, r["tin"], r["lin"])
-        if n == 1:
-            weights_third()
-        finish_all(passed)
-
-        def put_opp(cols, v):
+        ffn(k, widths[n], 1, 2, put)
+
+    def pass_on(n):
+        finish_all(gathers[order[n]])
+        passed[n] = forward(order[n])
+
+    def far_rows(n):
+        k = order[n]
+        finish_all(passed[n])
+
+        def put(cols, v):
             sopp[k][:, :, cols] = v.astype(bf).reshape(2, 64, 256)
-        ffn(k, width, 3, 1, put_opp)
+        ffn(k, widths[n], 3, 1, put)
         opposite[k] = (send(sopp[k].at[0], ropp[k].at[0], r["ops"].at[k, 0], r["opr"].at[k, 0], right),
                        send(sopp[k].at[1], ropp[k].at[1], r["ops"].at[k, 1], r["opr"].at[k, 1], left))
+
+    own_rows(0)
+    pass_on(0)
+    gathers[order[2]] = gather_out(order[2])
+    side_rows(0)
+    own_rows(1)
+    pass_on(1)
+    side_rows(1)
+    far_rows(0)
+    weights_second()
+    finish_all(hand)
+    student = dot(place, r["incoming"][...].reshape(256, 512).astype(bf)).astype(bf)
+    r["student"][...] = student
+    shared["in"] = share_rows(0, student, 16, r["tin"], r["lin"])
+    own_rows(2)
+    pass_on(2)
+    side_rows(2)
+    far_rows(1)
+    send_sides(order[0])
+    far_rows(2)
     send_sides(order[1])
+    weights_third()
     finish_all(stage3)
     student = r["student"][...]
     pre_act = dot(student, full[0][...].reshape(512, 1536))
@@ -302,16 +340,17 @@
         return jnp.concatenate(tiles, axis=0)
 
     def products(n, a, store):
-        heads = block_rows(r["lfeat"], a)
+        heads = block_rows(r["lfeat"], a) if n < 3 else None
         if n < 2:
             _, width, start = TEACHERS[n]
             store(GROUP_COLUMNS[n][0], dot(heads, rerr[:, start:start + width]).reshape(4, 16, width))
-        else:
-            store(2304, dot(block_rows(r["lin"], a), rpre[...]).reshape(4, 16, 1536))
-            store(3840, dot(heads, rerr[:, WH:WH + WB]).reshape(4, 16, WB))
+        elif n == 2:
+            store(2304, dot(heads, rerr[:, WH:WH + WB]).reshape(4, 16, WB))
             outs = dot(block_rows(r["lact"], a), rfg[...]).reshape(4, 48, 512)
             for m in range(3):
-                store(4608 + 512 * m, outs[:, 16 * m:16 * m + 16])
+                store(3072 + 512 * m, outs[:, 16 * m:16 * m + 16])
+        else:
+            store(4608, dot(block_rows(r["lin"], a), rpre[...]).reshape(4, 16, 1536))
 
     phase1, phase2 = {}, {}
 
@@ -367,34 +406,49 @@
     late = [cp, pair_send(6, rfg.at[pl.ds(0, 128)], rfg.at[pl.ds(128, 128)])]
     act_grad = dot_t(feat_grad, full[1][...].reshape(1536, 512))
     rpre[0:128] = (act_grad * r["slope"][...]).astype(bf)
-    late.append(pair_send(7, rpre.at[pl.ds(0, 128)], rpre.at[pl.ds(128, 128)]))
+    cp = pair_send(7, rpre.at[pl.ds(0, 128)], rpre.at[pl.ds(128, 128)])
     finish_all(late)
     start_group(2)
+    cp.wait()
+    start_group(3)
+
+    summed = {}
+
+    def send_sums(q):
+        start, width = SUM_COLUMNS[q]
+        cols, ref_cols = slice(start, start + width), pl.ds(start, width)
+        total = r["own2"][:, cols]
+        for i in range(3):
+            total = total + r["recv2"][i, :, cols].astype(f32)
+        r["sums"][y, :, cols] = total.astype(bf)
+        mine = r["sums"].at[y, :, ref_cols]
+        summed[q] = [send(mine, mine, r["s3s"].at[q, d - 1], r["s3r"].at[q, d - 1], at_y(y + d)) for d in (2, 1, 3)]
+
+    def sum_of(start, width):
+        cols = slice(start, start + width)
+        total = r["sums"][0, :, cols].astype(f32)
+        for t in range(1, 4):
+            total = total + r["sums"][t, :, cols].astype(f32)
+        return total
+
     next_group(1)
+    finish_all(phase2[0])
+    send_sums(0)
     next_group(2)
-    for n in range(3):
-        finish_all(phase2[n])
-    total = r["own2"][...]
-    for i in range(3):
-        total = total + r["recv2"][i].astype(f32)
-    r["own2"][...] = total
-    for t in range(4):
-        r["send3"][t] = total[:, 1536 * t:1536 * t + 1536].astype(bf)
-    copies = []
-    for d in (2, 1, 3):
-        t = (y + d) % 4
-        copies.append(send(r["send3"].at[t], r["recv3"].at[d - 1], r["s3s"].at[d - 1], r["s3r"].at[d - 1], at_y(t)))
-    finish_all(copies)
-    final = r["own2"][:, pl.ds(pl.multiple_of(y * 1536, 1536), 1536)]
-    for i in range(3):
-        final = final + r["recv3"][i].astype(f32)
-    r["mine3"][...] = final
-    out[y] = final
-    copies = []
-    for d in (2, 1, 3):
-        t = (y + d) % 4
-        copies.append(send(r["mine3"], out.at[y], r["s4s"].at[d - 1], r["s4r"].at[d - 1], at_y(t)))
-    finish_all(copies)
+    finish_all(phase2[1])
+    next_group(3)
+    finish_all(phase2[2])
+    send_sums(1)
+    finish_all(summed[0])
+    grad_head[:, WH + WB:] = sum_of(0, 1024)
+    finish_all(phase2[3])
+    send_sums(2)
+    finish_all(summed[1])
+    grad_head[:, 0:WH + WB] = sum_of(1024, 2048)
+    for m in range(3):
+        grad_out[16 * m:16 * m + 16] = sum_of(3072 + 512 * m, 512)
+    finish_all(summed[2])
+    grad_in[...] = sum_of(4608, 1536)
 
 
 def body(
@@ -405,11 +459,13 @@
     vm = pl.BlockSpec(memory_space=pltpu.VMEM)
     hbm = pl.BlockSpec(memory_space=pl.ANY)
     plan = scratch_plan()
-    out = pl.pallas_call(
+    f32 = jnp.float32
+    return tuple(pl.pallas_call(
         functools.partial(step_kernel, tuple(plan)),
-        out_shape=jax.ShapeDtypeStruct((4, 16, 1536), jnp.float32),
-        in_specs=[vm] * 3 + [hbm] * 6 + [vm] * 5 + [pl.BlockSpec(memory_space=pltpu.SMEM)],
-        out_specs=vm,
+        out_shape=[jax.ShapeDtypeStruct((16, 1536), f32), jax.ShapeDtypeStruct((48, 512), f32),
+                   jax.ShapeDtypeStruct((16, 3072), f32)],
+        in_specs=[hbm] * 14 + [pl.BlockSpec(memory_space=pltpu.SMEM)],
+        out_specs=[vm] * 3,
         scratch_shapes=list(plan.values()),
         compiler_params=pltpu.CompilerParams(
             collective_id=0, has_side_effects=True, vmem_limit_bytes=60 * 1024 * 1024),
@@ -417,12 +473,7 @@
         hid_whisper, hid_beats, hid_wavlm,
         up_whisper, down_whisper, up_beats, down_beats, up_wavlm, down_wavlm,
         w_in, w_out, w_head, student_in, send_counts[0], clip_len,
-    )
-    flat = out.transpose(1, 0, 2).reshape(16, SPAN)
-    grad_in = flat[:, 2304:3840]
-    grad_out = flat[:, 4608:].reshape(16, 3, 512).transpose(1, 0, 2).reshape(48, 512)
-    grad_head = jnp.concatenate([flat[:, 1024:2304], flat[:, 3840:4608], flat[:, 0:1024]], axis=1)
-    return grad_in, grad_out, grad_head
+    ))
 
 
 def solution(mesh):

time: 105 us -> 99.5 us (0.948)
  Pallas kernels: 100 us -> 93.3 us
  local copies, waits for them, and re-layouts: 2.44 us -> 4.69 us
    pallas_call x1, Pallas kernels: 100 us -> 93.3 us  [body(): pl.pallas_call(functools.partial(step_kernel, tuple(plan)), out_shape=[ja...]
    unnamed x0 -> x3, local copies, waits for them, and re-layouts: none -> 4.69 us
    reshape x2 -> x0, local copies, waits for them, and re-layouts: 1.1 us -> none  [the longest x1 1.02 us: body(): flat = out.transpose(1, 0, 2).reshape(16, SPAN)]
where the time goes in v4:
time: 99.5 us; the launch traced here: 99.3 us
  Pallas kernels  93.3 us (94%)
  local copies, waits for them, and re-layouts  4.69 us (5%)
  between operations  1.29 us (1%)
    pallas_call x1, Pallas kernels, body(): pl.pallas_call(functools.partial(step_kernel, tuple(plan)), out_shape=[ja...  93.3 us
    unnamed x3, local copies, waits for them, and re-layouts  4.69 us

profile of v4, /device:TPU:0, one launch (start us, length us, event | category | flops | bytes accessed | tf_op | source)
XLA Modules:
  0.0 99.3 jit_solution(11260197887534735023)
XLA Ops:
  1.3 93.3 %shard_map.166 = (f32[16,1536]{1,0:T(8,128)}, f32[48,512]{1,0:T(8,128)}, f32[16,3072]{1,0:T(8,128)}) custom-call(bf16[128,1280]{1,0:T(8,128)(2,1)} %refs_0_.1, bf16[128,768]{1,0:T(8,128)(2,1)} %refs_1_.1, bf16[128,1024]{1,0:T(8,128)(2,1)} %refs_2_.1, bf16[1280,1280]{1,0:T(8,128)(2,1)} %refs_3_.1, bf16[1280,1280]{1,0:T(8,128)(2,1)} %refs_4_.1, ...), custom_call_target="tpu_custom_call" | custom-call | tf_op jit(solution)/shard_map/pallas_call | solution.py:463
  94.6 1.5 %copy.22 = f32[16,1536]{1,0:T(8,128)} copy(f32[16,1536]{1,0:T(8,128)} %get-tuple-element.6) | data formatting | bytes 196608
  96.1 1.5 %copy.23 = f32[48,512]{1,0:T(8,128)} copy(f32[48,512]{1,0:T(8,128)} %get-tuple-element.7) | data formatting | bytes 196608
  97.7 1.6 %copy.24 = f32[16,3072]{1,0:T(8,128)} copy(f32[16,3072]{1,0:T(8,128)} %get-tuple-element.8) | data formatting | bytes 393216

commit v5 on v4

--- a/solution.py
+++ b/solution.py
@@ -47,8 +47,9 @@
         plan[f"hid{k}"] = vm((128, w), bf)
         plan[f"vup{k}"] = vm((w, w), bf)
         plan[f"vdown{k}"] = vm((w, w), bf)
-        plan[f"normed{k}"] = vm((4, 128, w), bf)
         plan[f"keep{k}"] = vm((128, w), f32)
+        plan[f"normed{k}"] = vm((1 if k == 1 else 4, 128, w), bf)
+    for k, w in ((0, WH), (2, WL)):
         plan[f"part{k}"] = vm((2, 128, w), f32)
         plan[f"sopp{k}"] = vm((2, 64, w), bf)
         plan[f"ropp{k}"] = vm((2, 64, w), bf)
@@ -66,12 +67,12 @@
         rpre=vm((256, 1536), bf), rfg=vm((256, 512), bf), rerr=vm((256, 3072), bf),
         own1=vm((4, 16, SPAN), f32), send1=vm((3, 4, 16, SPAN), bf), recv1=vm((3, 4, 16, SPAN), bf),
         own2=vm((16, SPAN), f32), send2=vm((3, 16, SPAN), bf), recv2=vm((3, 16, SPAN), bf),
-        sums=vm((4, 16, SPAN), bf),
         rows_in=vm((128, 512), bf), counts=vm((32, 32), jnp.int32),
         wsem=dma((6,)), isem=dma((8,)),
         ags=dma((3, 2)), agr=dma((3, 2)), fws=dma((3, 2)), fwr=dma((3, 2)),
         ops=dma((3, 2)), opr=dma((3, 2)), sds=dma((3, 2)), sdr=dma((3, 2)),
-        w1s=dma((3, 3)), w1r=dma((3, 3)), w2s=dma((3, 3, 4)), w2r=dma((3, 3, 4)), w3s=dma((3,)), w3r=dma((3,)),
+        piece=vm((2, 48, WB), bf), others=vm((2, 4, 4, 3, 48, WB), bf),
+        psem=dma((2,)), pys=dma((3,)), pyr=dma((3,)), gs=dma((96,)), gr=dma((96,)),
         hos=dma((32,)), hor=dma((32,)),
         xs=dma((8,)), xr=dma((8,)),
         s1s=dma((4, 3)), s1r=dma((4, 3)), s2s=dma((4, 3)), s2r=dma((4, 3)), s3s=dma((3, 3)), s3r=dma((3, 3)),
@@ -85,9 +86,9 @@
 def step_kernel(names, *refs):
     ups, downs = refs[3:9:2], refs[4:9:2]
     shards = refs[9:12]
-    clip_ref, grad_in, grad_out, grad_head = refs[14:18]
-    r = dict(zip(names, refs[18:]))
-    per = lambda name: [r[f"{name}{k}"] for k in range(3)]
+    clip_ref, sums = refs[14:16]
+    r = dict(zip(names, refs[16:]))
+    per = lambda name: [r.get(f"{name}{k}") for k in range(3)]
     hid = per("hid")
     vup, vdown, normed, keep, part = per("vup"), per("vdown"), per("normed"), per("keep"), per("part")
     sopp, ropp, sside, rside, full = per("sopp"), per("ropp"), per("sside"), per("rside"), per("full")
@@ -137,6 +138,11 @@
     )):
         ready[name] = pltpu.make_async_copy(src, dst, r["isem"].at[i])
         ready[name].start()
+    piece_rows = pl.ds(pl.multiple_of((x * 4 + z) * 48, 48), 48)
+    pieces = [pltpu.make_async_copy(src.at[piece_rows], r["piece"].at[i], r["psem"].at[i])
+              for i, src in enumerate((ups[1], downs[1]))]
+    for cp in pieces:
+        cp.start()
     loads = {}
     for n, (k, _, _) in enumerate(TEACHERS):
         loads[k] = (pltpu.make_async_copy(ups[k], vup[k], r["wsem"].at[2 * n]),
@@ -200,36 +206,97 @@
             cols = slice(256 * j, 256 * j + 256)
             store(cols, dot(hidden[0:rows, 0:width], vdown[k][:, cols]))
 
+    counter = iter(range(96))
+    others = r["others"]
+
+    def ring_send(ref, dev):
+        i = next(counter)
+        return send(ref, ref, r["gs"].at[i], r["gr"].at[i], dev)
+
+    def slot_of(f, s):
+        return jnp.where(swap, s, f), jnp.where(swap, f, s)
+
+    def student_slot(f, s):
+        i, j = slot_of(f, s)
+        return [full[m].at[i, j, c] for m in range(3)]
+
+    def beats_slot(f, s):
+        i, j = slot_of(f, s)
+        return others.at[c, i, j]
+
+    up1, down1 = (first + 1) % 4, (first + 3) % 4
+    up2, down2 = (second + 1) % 4, (second + 3) % 4
+    up1_dev, down1_dev, up2_dev, down2_dev = at_first(up1), at_first(down1), at_second(up2), at_second(down2)
+
     gathers = {order[0]: gather_out(order[0])}
+    stage = {}
+    stage["s1"] = [ring_send(ref, dev) for ref in student_slot(first, second) for dev in (up1_dev, down1_dev)]
+    finish_all(pieces)
+    stage["py"] = [send(r["piece"].at[c], others.at[c, x, z, 3 - o], r["pys"].at[o - 1], r["pyr"].at[o - 1], at_y(y + o))
+                   for o in (2, 1, 3)]
+    ready[order[1]].wait()
+    normed[order[1]][0] = layer_norm(hid[order[1]][...]).astype(bf)
+    gathers[order[1]] = gather_out(order[1])
     hand = []
     for d in range(1, 32):
         to = (dp + d) % 32
         hand.append(send(r["outgoing"].at[to], r["incoming"].at[dp], r["hos"].at[d], r["hor"].at[d], {"dp": to}))
-    stage1 = []
-    for d in (2, 1, 3):
-        for m in range(3):
-            stage1.append(send(full[m].at[x, z, c], full[m].at[x, z, c], r["w1s"].at[d - 1, m], r["w1r"].at[d - 1, m],
-                               at_first((first + d) % 4)))
-    for k in order[1:]:
-        ready[k].wait()
-        normed[k][0] = layer_norm(hid[k][...]).astype(bf)
-    gathers[order[1]] = gather_out(order[1])
-    stage2, stage3 = [], []
-
-    def weights_second():
-        finish_all(stage1)
-        for d in (2, 1, 3):
-            dev = at_second((second + d) % 4)
-            for m in range(3):
-                for i in range(4):
-                    place_at = full[m].at[jnp.where(swap, x, i), jnp.where(swap, i, z), c]
-                    stage2.append(send(place_at, place_at, r["w2s"].at[d - 1, m, i], r["w2r"].at[d - 1, m, i], dev))
-
-    def weights_third():
-        finish_all(stage2)
-        for m in range(3):
-            half = full[m].at[:, :, c]
-            stage3.append(send(half, half, r["w3s"].at[m], r["w3r"].at[m], pair))
+    ready[order[2]].wait()
+    normed[order[2]][0] = layer_norm(hid[order[2]][...]).astype(bf)
+
+    def student_first_forward():
+        finish_all(stage["s1"])
+        low, high = student_slot(down1, second), student_slot(up1, second)
+        stage["s1f"] = [ring_send(low[2], up1_dev), ring_send(high[0], down1_dev), ring_send(high[1], down1_dev)]
+
+    def student_second():
+        finish_all(stage["s1f"])
+        stage["s2"] = [ring_send(ref, dev) for i in range(4) for ref in student_slot(i, second)
+                       for dev in (up2_dev, down2_dev)]
+
+    def student_second_forward():
+        finish_all(stage["s2"])
+        stage["s2f"] = [ring_send(ref, up2_dev) for i in (0, 1) for ref in student_slot(i, down2)]
+        stage["s2f"] += [ring_send(ref, down2_dev) for i in (2, 3) for ref in student_slot(i, up2)]
+
+    def student_pair():
+        finish_all(stage["s2f"])
+        stage["s3"] = [ring_send(full[m].at[:, :, c], pair) for m in range(3)]
+
+    def beats_first():
+        finish_all(stage["py"])
+        stage["b1"] = [ring_send(beats_slot(first, second), dev) for dev in (up1_dev, down1_dev)]
+
+    def beats_first_forward():
+        finish_all(stage["b1"])
+        stage["b1f"] = [ring_send(beats_slot(down1, second).at[pl.ds(0, 2)], up1_dev),
+                        ring_send(beats_slot(up1, second).at[pl.ds(2, 1)], down1_dev)]
+
+    def beats_second():
+        finish_all(stage["b1f"])
+        stage["b2"] = [ring_send(beats_slot(i, second), dev) for i in range(4) for dev in (up2_dev, down2_dev)]
+        stage["b3"] = [ring_send(beats_slot(i, second), pair) for i in range(4)]
+
+    def beats_second_forward():
+        finish_all(stage["b2"])
+        stage["b2f"] = [ring_send(beats_slot(i, down2), up2_dev) for i in (0, 1)]
+        stage["b2f"] += [ring_send(beats_slot(i, up2), down2_dev) for i in (2, 3)]
+        stage["b3"] += [ring_send(beats_slot(i, s), pair) for s in (down2, up2) for i in range(4)]
+
+    def beats_pair():
+        finish_all(stage["b2f"])
+        stage["b3"] += [ring_send(beats_slot(i, (second + 2) % 4), pair) for i in range(4)]
+        finish_all(stage["b3"])
+
+    def beats_rest():
+        values = normed[1][0]
+        for d in range(3):
+            for j in range(WB // 256):
+                cols = slice(256 * j, 256 * j + 256)
+                hidden[0:128, cols] = gelu(dot(values, others[0, :, :, d, :, cols].reshape(WB, 256))).astype(bf)
+            for j in range(WB // 256):
+                cols = slice(256 * j, 256 * j + 256)
+                keep[1][:, cols] += dot(hidden[0:128, 0:WB], others[1, :, :, d, :, cols].reshape(WB, 256))
 
     opposite, sides = {}, {}
 
@@ -283,27 +350,29 @@
                        send(sopp[k].at[1], ropp[k].at[1], r["ops"].at[k, 1], r["opr"].at[k, 1], left))
 
     own_rows(0)
+    student_first_forward()
     pass_on(0)
-    gathers[order[2]] = gather_out(order[2])
+    own_rows(1)
+    student_second()
+    beats_first()
     side_rows(0)
-    own_rows(1)
     pass_on(1)
     side_rows(1)
+    beats_first_forward()
     far_rows(0)
-    weights_second()
+    student_second_forward()
+    beats_second()
     finish_all(hand)
     student = dot(place, r["incoming"][...].reshape(256, 512).astype(bf)).astype(bf)
     r["student"][...] = student
     shared["in"] = share_rows(0, student, 16, r["tin"], r["lin"])
     own_rows(2)
-    pass_on(2)
-    side_rows(2)
     far_rows(1)
     send_sides(order[0])
-    far_rows(2)
+    student_pair()
     send_sides(order[1])
-    weights_third()
-    finish_all(stage3)
+    finish_all(stage["s3"])
+    beats_second_forward()
     student = r["student"][...]
     pre_act = dot(student, full[0][...].reshape(512, 1536))
     shifted = pre_act - 4.0
@@ -311,7 +380,6 @@
     activated = (soft - 0.08 * pre_act - 0.035).astype(bf)
     r["slope"][...] = jax.nn.sigmoid(shifted) - 0.08
     features = (student.astype(f32) + dot(activated, full[1][...].reshape(1536, 512))).astype(bf)
-    send_sides(order[2])
     shared["feat"] = share_rows(1, features, 16, r["tfeat"], r["lfeat"])
     shared["act"] = share_rows(2, activated, 48, r["tact"], r["lact"])
     for k, width, start in TEACHERS:
@@ -320,8 +388,10 @@
     def error_of(n):
         k, width, start = TEACHERS[n]
         cols = slice(start, start + width)
-        finish_all(sides[k])
-        total = hid[k][...].astype(f32) + keep[k][...] + rside[k][0].astype(f32) + rside[k][1].astype(f32)
+        total = hid[k][...].astype(f32) + keep[k][...]
+        if n < 2:
+            finish_all(sides[k])
+            total = total + rside[k][0].astype(f32) + rside[k][1].astype(f32)
         target = total.astype(bf).astype(f32)
         err = ((r["predicted"][:, cols] - target) * (2.0 / width) * mask).astype(bf)
         rerr[0:128, cols] = err
@@ -395,6 +465,8 @@
     cp, _ = error_of(0)
     finish_all([cp, shared["feat"]])
     start_group(0)
+    beats_pair()
+    beats_rest()
     cp, _ = error_of(1)
     cp.wait()
     start_group(1)
@@ -420,16 +492,9 @@
         total = r["own2"][:, cols]
         for i in range(3):
             total = total + r["recv2"][i, :, cols].astype(f32)
-        r["sums"][y, :, cols] = total.astype(bf)
-        mine = r["sums"].at[y, :, ref_cols]
+        sums[y, :, cols] = total.astype(bf)
+        mine = sums.at[y, :, ref_cols]
         summed[q] = [send(mine, mine, r["s3s"].at[q, d - 1], r["s3r"].at[q, d - 1], at_y(y + d)) for d in (2, 1, 3)]
-
-    def sum_of(start, width):
-        cols = slice(start, start + width)
-        total = r["sums"][0, :, cols].astype(f32)
-        for t in range(1, 4):
-            total = total + r["sums"][t, :, cols].astype(f32)
-        return total
 
     next_group(1)
     finish_all(phase2[0])
@@ -439,15 +504,24 @@
     next_group(3)
     finish_all(phase2[2])
     send_sums(1)
-    finish_all(summed[0])
-    grad_head[:, WH + WB:] = sum_of(0, 1024)
     finish_all(phase2[3])
     send_sums(2)
-    finish_all(summed[1])
+    for q in range(3):
+        finish_all(summed[q])
+
+
+def sum_kernel(sums, grad_in, grad_out, grad_head):
+    def sum_of(start, width):
+        cols = slice(start, start + width)
+        total = sums[0, :, cols].astype(jnp.float32)
+        for t in range(1, 4):
+            total = total + sums[t, :, cols].astype(jnp.float32)
+        return total
+
+    grad_head[:, WH + WB:] = sum_of(0, 1024)
     grad_head[:, 0:WH + WB] = sum_of(1024, 2048)
     for m in range(3):
         grad_out[16 * m:16 * m + 16] = sum_of(3072 + 512 * m, 512)
-    finish_all(summed[2])
     grad_in[...] = sum_of(4608, 1536)
 
 
@@ -460,20 +534,26 @@
     hbm = pl.BlockSpec(memory_space=pl.ANY)
     plan = scratch_plan()
     f32 = jnp.float32
-    return tuple(pl.pallas_call(
+    sums = pl.pallas_call(
         functools.partial(step_kernel, tuple(plan)),
-        out_shape=[jax.ShapeDtypeStruct((16, 1536), f32), jax.ShapeDtypeStruct((48, 512), f32),
-                   jax.ShapeDtypeStruct((16, 3072), f32)],
+        out_shape=jax.ShapeDtypeStruct((4, 16, SPAN), jnp.bfloat16),
         in_specs=[hbm] * 14 + [pl.BlockSpec(memory_space=pltpu.SMEM)],
-        out_specs=[vm] * 3,
+        out_specs=vm,
         scratch_shapes=list(plan.values()),
         compiler_params=pltpu.CompilerParams(
-            collective_id=0, has_side_effects=True, vmem_limit_bytes=60 * 1024 * 1024),
+            collective_id=0, has_side_effects=True, vmem_limit_bytes=62 * 1024 * 1024),
     )(
         hid_whisper, hid_beats, hid_wavlm,
         up_whisper, down_whisper, up_beats, down_beats, up_wavlm, down_wavlm,
         w_in, w_out, w_head, student_in, send_counts[0], clip_len,
-    ))
+    )
+    return tuple(pl.pallas_call(
+        sum_kernel,
+        out_shape=[jax.ShapeDtypeStruct((16, 1536), f32), jax.ShapeDtypeStruct((48, 512), f32),
+                   jax.ShapeDtypeStruct((16, 3072), f32)],
+        in_specs=[vm],
+        out_specs=[vm] * 3,
+    )(sums))
 
 
 def solution(mesh):

time: 99.5 us -> 103 us (1.035)
  Pallas kernels: 93.3 us -> 102 us
  local copies, waits for them, and re-layouts: 4.69 us -> 0 us
    pallas_call x1 -> x2, Pallas kernels: 93.3 us -> 102 us  [the longest x1 99.6 us: body(): pl.pallas_call(functools.partial(step_kernel, tuple(plan)), out_shape=jax...]
    unnamed x3 -> x0, local copies, waits for them, and re-layouts: 4.69 us -> none
where the time goes in v5:
time: 103 us
  Pallas kernels  102 us (99%)
  between operations  1.29 us (1%)
    pallas_call x1, Pallas kernels, body(): pl.pallas_call(functools.partial(step_kernel, tuple(plan)), out_shape=jax...  99.6 us

profile of v5, /device:TPU:0, one launch (start us, length us, event | category | flops | bytes accessed | tf_op | source)
XLA Modules:
  0.0 102.8 jit_solution(1924523529079955368)
XLA Ops:
  1.3 99.6 %shard_map.166.sums = bf16[4,16,6144]{2,1,0:T(8,128)(2,1)} custom-call(bf16[128,1280]{1,0:T(8,128)(2,1)} %refs_0_.1, bf16[128,768]{1,0:T(8,128)(2,1)} %refs_1_.1, bf16[128,1024]{1,0:T(8,128)(2,1)} %refs_2_.1, bf16[1280,1280]{1,0:T(8,128)(2,1)} %refs_3_.1, bf16[1280,1280]{1,0:T(8,128)(2,1)} %refs_4_.1, bf16[768,768]{1,0:T(8,128)(2,1)} %refs_5_.1, ...), custom_call_target="tpu_custom_call" | custom-call | tf_op jit(solution)/shard_map/pallas_call | solution.py:537
  100.9 1.9 %shard_map.167 = (f32[16,1536]{1,0:T(8,128)}, f32[48,512]{1,0:T(8,128)}, f32[16,3072]{1,0:T(8,128)}) custom-call(bf16[4,16,6144]{2,1,0:T(8,128)(2,1)} %shard_map.166.sums), custom_call_target="tpu_custom_call" | custom-call | tf_op jit(solution)/shard_map/pallas_call | solution.py:550

commit v6 on v5

--- a/solution.py
+++ b/solution.py
@@ -224,13 +224,13 @@
         i, j = slot_of(f, s)
         return others.at[c, i, j]
 
-    up1, down1 = (first + 1) % 4, (first + 3) % 4
     up2, down2 = (second + 1) % 4, (second + 3) % 4
-    up1_dev, down1_dev, up2_dev, down2_dev = at_first(up1), at_first(down1), at_second(up2), at_second(down2)
+    up2_dev, down2_dev = at_second(up2), at_second(down2)
+    row_devs = [at_first((first + d) % 4) for d in (2, 1, 3)]
 
     gathers = {order[0]: gather_out(order[0])}
     stage = {}
-    stage["s1"] = [ring_send(ref, dev) for ref in student_slot(first, second) for dev in (up1_dev, down1_dev)]
+    stage["s1"] = [ring_send(ref, dev) for dev in row_devs for ref in student_slot(first, second)]
     finish_all(pieces)
     stage["py"] = [send(r["piece"].at[c], others.at[c, x, z, 3 - o], r["pys"].at[o - 1], r["pyr"].at[o - 1], at_y(y + o))
                    for o in (2, 1, 3)]
@@ -244,49 +244,45 @@
     ready[order[2]].wait()
     normed[order[2]][0] = layer_norm(hid[order[2]][...]).astype(bf)
 
-    def student_first_forward():
+    def spread_second(name, slots):
+        stage[name + "a"], stage[name + "b"] = [], []
+        for part, ups_first in ((name + "a", ((0, 2), (1, 3))), (name + "b", ((2, 0), (3, 1)))):
+            for i, j in ups_first:
+                stage[part] += [ring_send(ref, up2_dev) for ref in slots(i, second)]
+                stage[part] += [ring_send(ref, down2_dev) for ref in slots(j, second)]
+
+    def relay_second(name, slots):
+        finish_all(stage[name + "a"])
+        stage[name + "f"] = [ring_send(ref, up2_dev) for i in (0, 1) for ref in slots(i, down2)]
+        stage[name + "f"] += [ring_send(ref, down2_dev) for i in (2, 3) for ref in slots(i, up2)]
+
+    def student_second():
         finish_all(stage["s1"])
-        low, high = student_slot(down1, second), student_slot(up1, second)
-        stage["s1f"] = [ring_send(low[2], up1_dev), ring_send(high[0], down1_dev), ring_send(high[1], down1_dev)]
-
-    def student_second():
-        finish_all(stage["s1f"])
-        stage["s2"] = [ring_send(ref, dev) for i in range(4) for ref in student_slot(i, second)
-                       for dev in (up2_dev, down2_dev)]
-
-    def student_second_forward():
-        finish_all(stage["s2"])
-        stage["s2f"] = [ring_send(ref, up2_dev) for i in (0, 1) for ref in student_slot(i, down2)]
-        stage["s2f"] += [ring_send(ref, down2_dev) for i in (2, 3) for ref in student_slot(i, up2)]
+        spread_second("s2", student_slot)
 
     def student_pair():
-        finish_all(stage["s2f"])
+        finish_all(stage["s2b"] + stage["s2f"])
         stage["s3"] = [ring_send(full[m].at[:, :, c], pair) for m in range(3)]
+
+    def beats_slots(f, s):
+        return [beats_slot(f, s)]
 
     def beats_first():
         finish_all(stage["py"])
-        stage["b1"] = [ring_send(beats_slot(first, second), dev) for dev in (up1_dev, down1_dev)]
-
-    def beats_first_forward():
+        stage["b1"] = [ring_send(beats_slot(first, second), dev) for dev in row_devs]
+
+    def beats_second():
         finish_all(stage["b1"])
-        stage["b1f"] = [ring_send(beats_slot(down1, second).at[pl.ds(0, 2)], up1_dev),
-                        ring_send(beats_slot(up1, second).at[pl.ds(2, 1)], down1_dev)]
-
-    def beats_second():
-        finish_all(stage["b1f"])
-        stage["b2"] = [ring_send(beats_slot(i, second), dev) for i in range(4) for dev in (up2_dev, down2_dev)]
+        spread_second("b2", beats_slots)
         stage["b3"] = [ring_send(beats_slot(i, second), pair) for i in range(4)]
 
-    def beats_second_forward():
-        finish_all(stage["b2"])
-        stage["b2f"] = [ring_send(beats_slot(i, down2), up2_dev) for i in (0, 1)]
-        stage["b2f"] += [ring_send(beats_slot(i, up2), down2_dev) for i in (2, 3)]
+    def beats_share():
+        finish_all(stage["b2b"])
         stage["b3"] += [ring_send(beats_slot(i, s), pair) for s in (down2, up2) for i in range(4)]
 
     def beats_pair():
         finish_all(stage["b2f"])
         stage["b3"] += [ring_send(beats_slot(i, (second + 2) % 4), pair) for i in range(4)]
-        finish_all(stage["b3"])
 
     def beats_rest():
         values = normed[1][0]
@@ -350,29 +346,27 @@
                        send(sopp[k].at[1], ropp[k].at[1], r["ops"].at[k, 1], r["opr"].at[k, 1], left))
 
     own_rows(0)
-    student_first_forward()
+    student_second()
     pass_on(0)
     own_rows(1)
-    student_second()
+    side_rows(0)
+    own_rows(2)
     beats_first()
-    side_rows(0)
     pass_on(1)
     side_rows(1)
-    beats_first_forward()
+    relay_second("s2", student_slot)
     far_rows(0)
-    student_second_forward()
     beats_second()
     finish_all(hand)
     student = dot(place, r["incoming"][...].reshape(256, 512).astype(bf)).astype(bf)
     r["student"][...] = student
     shared["in"] = share_rows(0, student, 16, r["tin"], r["lin"])
-    own_rows(2)
     far_rows(1)
     send_sides(order[0])
     student_pair()
+    relay_second("b2", beats_slots)
     send_sides(order[1])
     finish_all(stage["s3"])
-    beats_second_forward()
     student = r["student"][...]
     pre_act = dot(student, full[0][...].reshape(512, 1536))
     shifted = pre_act - 4.0
@@ -382,6 +376,7 @@
     features = (student.astype(f32) + dot(activated, full[1][...].reshape(1536, 512))).astype(bf)
     shared["feat"] = share_rows(1, features, 16, r["tfeat"], r["lfeat"])
     shared["act"] = share_rows(2, activated, 48, r["tact"], r["lact"])
+    beats_share()
     for k, width, start in TEACHERS:
         r["predicted"][:, start:start + width] = dot(features, full[2][:, :, :, :, start:start + width].reshape(512, width))
 
@@ -466,12 +461,13 @@
     finish_all([cp, shared["feat"]])
     start_group(0)
     beats_pair()
-    beats_rest()
     cp, _ = error_of(1)
+    finish_all([shared["in"], shared["act"]])
+    next_group(0)
     cp.wait()
     start_group(1)
-    finish_all([shared["in"], shared["act"]])
-    next_group(0)
+    finish_all(stage["b3"])
+    beats_rest()
     cp, back = error_of(2)
     feat_grad = back.astype(bf)
     rfg[0:128] = feat_grad

time: 103 us -> 95.3 us (0.925)
  Pallas kernels: 102 us -> 93.1 us
    pallas_call x1, Pallas kernels: 99.6 us -> 91.2 us  [body(): pl.pallas_call(functools.partial(step_kernel, tuple(plan)), out_shape=jax...]
where the time goes in v6:
time: 95.3 us; the launch traced here: 94.4 us
  Pallas kernels  93.1 us (98%)
  between operations  1.29 us (1%)
    pallas_call x1, Pallas kernels, body(): pl.pallas_call(functools.partial(step_kernel, tuple(plan)), out_shape=jax...  91.2 us
    pallas_call x1, Pallas kernels, body(): pl.pallas_call(sum_kernel, out_shape=[jax.ShapeDtypeStruct((16, 1536), f3...  1.91 us

profile of v6, /device:TPU:0, one launch (start us, length us, event | category | flops | bytes accessed | tf_op | source)
XLA Modules:
  0.0 94.4 jit_solution(1921809140409754388)
XLA Ops:
  1.3 91.2 %shard_map.166.sums = bf16[4,16,6144]{2,1,0:T(8,128)(2,1)} custom-call(bf16[128,1280]{1,0:T(8,128)(2,1)} %refs_0_.1, bf16[128,768]{1,0:T(8,128)(2,1)} %refs_1_.1, bf16[128,1024]{1,0:T(8,128)(2,1)} %refs_2_.1, bf16[1280,1280]{1,0:T(8,128)(2,1)} %refs_3_.1, bf16[1280,1280]{1,0:T(8,128)(2,1)} %refs_4_.1, bf16[768,768]{1,0:T(8,128)(2,1)} %refs_5_.1, ...), custom_call_target="tpu_custom_call" | custom-call | tf_op jit(solution)/shard_map/pallas_call | solution.py:533
  92.5 1.9 %shard_map.167 = (f32[16,1536]{1,0:T(8,128)}, f32[48,512]{1,0:T(8,128)}, f32[16,3072]{1,0:T(8,128)}) custom-call(bf16[4,16,6144]{2,1,0:T(8,128)(2,1)} %shard_map.166.sums), custom_call_target="tpu_custom_call" | custom-call | tf_op jit(solution)/shard_map/pallas_call | solution.py:546

commit v7 on v6

--- a/solution.py
+++ b/solution.py
@@ -24,7 +24,6 @@
 TEACHERS = ((2, WL, WH + WB), (0, WH, 0), (1, WB, WH))
 SPAN = 6144
 GROUP_COLUMNS = ((0, 1024), (1024, 1280), (2304, 2304), (4608, 1536))
-SUM_COLUMNS = ((0, 1024), (1024, 3584), (4608, 1536))
 
 
 def gelu(values):
@@ -75,7 +74,7 @@
         psem=dma((2,)), pys=dma((3,)), pyr=dma((3,)), gs=dma((96,)), gr=dma((96,)),
         hos=dma((32,)), hor=dma((32,)),
         xs=dma((8,)), xr=dma((8,)),
-        s1s=dma((4, 3)), s1r=dma((4, 3)), s2s=dma((4, 3)), s2r=dma((4, 3)), s3s=dma((3, 3)), s3r=dma((3, 3)),
+        s1s=dma((4, 3)), s1r=dma((4, 3)), s2s=dma((4, 3)), s2r=dma((4, 3)), s3s=dma((4, 3)), s3r=dma((4, 3)),
     )
     return plan
 
@@ -351,21 +350,19 @@
     own_rows(1)
     side_rows(0)
     own_rows(2)
+    relay_second("s2", student_slot)
     beats_first()
     pass_on(1)
     side_rows(1)
-    relay_second("s2", student_slot)
     far_rows(0)
-    beats_second()
+    student_pair()
     finish_all(hand)
     student = dot(place, r["incoming"][...].reshape(256, 512).astype(bf)).astype(bf)
     r["student"][...] = student
     shared["in"] = share_rows(0, student, 16, r["tin"], r["lin"])
     far_rows(1)
     send_sides(order[0])
-    student_pair()
-    relay_second("b2", beats_slots)
-    send_sides(order[1])
+    beats_second()
     finish_all(stage["s3"])
     student = r["student"][...]
     pre_act = dot(student, full[0][...].reshape(512, 1536))
@@ -374,9 +371,10 @@
     activated = (soft - 0.08 * pre_act - 0.035).astype(bf)
     r["slope"][...] = jax.nn.sigmoid(shifted) - 0.08
     features = (student.astype(f32) + dot(activated, full[1][...].reshape(1536, 512))).astype(bf)
+    send_sides(order[1])
     shared["feat"] = share_rows(1, features, 16, r["tfeat"], r["lfeat"])
     shared["act"] = share_rows(2, activated, 48, r["tact"], r["lact"])
-    beats_share()
+    relay_second("b2", beats_slots)
     for k, width, start in TEACHERS:
         r["predicted"][:, start:start + width] = dot(features, full[2][:, :, :, :, start:start + width].reshape(512, width))
 
@@ -458,6 +456,7 @@
         phase2[n] = copies
 
     cp, _ = error_of(0)
+    beats_share()
     finish_all([cp, shared["feat"]])
     start_group(0)
     beats_pair()
@@ -475,6 +474,7 @@
     act_grad = dot_t(feat_grad, full[1][...].reshape(1536, 512))
     rpre[0:128] = (act_grad * r["slope"][...]).astype(bf)
     cp = pair_send(7, rpre.at[pl.ds(0, 128)], rpre.at[pl.ds(128, 128)])
+    next_group(1)
     finish_all(late)
     start_group(2)
     cp.wait()
@@ -483,7 +483,7 @@
     summed = {}
 
     def send_sums(q):
-        start, width = SUM_COLUMNS[q]
+        start, width = GROUP_COLUMNS[q]
         cols, ref_cols = slice(start, start + width), pl.ds(start, width)
         total = r["own2"][:, cols]
         for i in range(3):
@@ -492,17 +492,17 @@
         mine = sums.at[y, :, ref_cols]
         summed[q] = [send(mine, mine, r["s3s"].at[q, d - 1], r["s3r"].at[q, d - 1], at_y(y + d)) for d in (2, 1, 3)]
 
-    next_group(1)
     finish_all(phase2[0])
     send_sums(0)
+    finish_all(phase2[1])
+    send_sums(1)
     next_group(2)
-    finish_all(phase2[1])
     next_group(3)
     finish_all(phase2[2])
-    send_sums(1)
+    send_sums(2)
     finish_all(phase2[3])
-    send_sums(2)
-    for q in range(3):
+    send_sums(3)
+    for q in range(4):
         finish_all(summed[q])
 
 

time: 95.3 us -> 99.6 us (1.045)
  Pallas kernels: 93.1 us -> 98.1 us
    pallas_call x1, Pallas kernels: 91.2 us -> 96.2 us  [body(): pl.pallas_call(functools.partial(step_kernel, tuple(plan)), out_shape=jax...]
where the time goes in v7:
time: 99.6 us; the launch traced here: 99.4 us
  Pallas kernels  98.1 us (98%)
  between operations  1.29 us (1%)
    pallas_call x1, Pallas kernels, body(): pl.pallas_call(functools.partial(step_kernel, tuple(plan)), out_shape=jax...  96.2 us

profile of v7, /device:TPU:0, one launch (start us, length us, event | category | flops | bytes accessed | tf_op | source)
XLA Modules:
  0.0 99.4 jit_solution(16464833984130485471)
XLA Ops:
  1.3 96.2 %shard_map.166.sums = bf16[4,16,6144]{2,1,0:T(8,128)(2,1)} custom-call(bf16[128,1280]{1,0:T(8,128)(2,1)} %refs_0_.1, bf16[128,768]{1,0:T(8,128)(2,1)} %refs_1_.1, bf16[128,1024]{1,0:T(8,128)(2,1)} %refs_2_.1, bf16[1280,1280]{1,0:T(8,128)(2,1)} %refs_3_.1, bf16[1280,1280]{1,0:T(8,128)(2,1)} %refs_4_.1, bf16[768,768]{1,0:T(8,128)(2,1)} %refs_5_.1, ...), custom_call_target="tpu_custom_call" | custom-call | tf_op jit(solution)/shard_map/pallas_call | solution.py:533
  97.5 1.9 %shard_map.167 = (f32[16,1536]{1,0:T(8,128)}, f32[48,512]{1,0:T(8,128)}, f32[16,3072]{1,0:T(8,128)}) custom-call(bf16[4,16,6144]{2,1,0:T(8,128)(2,1)} %shard_map.166.sums), custom_call_target="tpu_custom_call" | custom-call | tf_op jit(solution)/shard_map/pallas_call | solution.py:546

commit v8 on v7

--- a/solution.py
+++ b/solution.py
@@ -59,7 +59,7 @@
     plan.update(
         hidden=vm((256, WH), bf),
         outgoing=vm((32, 8, 512), HAND), incoming=vm((32, 8, 512), HAND),
-        student=vm((128, 512), bf),
+        student=vm((128, 512), bf), active=vm((128, 1536), bf),
         slope=vm((128, 1536), f32), predicted=vm((128, 3072), f32), fgrad=vm((128, 512), f32),
         tin=vm((4, 4, 2, 16, 128), bf), tact=vm((4, 4, 2, 48, 128), bf), tfeat=vm((4, 4, 2, 16, 128), bf),
         lin=vm((4, 4, 16, 256), bf), lact=vm((4, 4, 48, 256), bf), lfeat=vm((4, 4, 16, 256), bf),
@@ -350,31 +350,35 @@
     own_rows(1)
     side_rows(0)
     own_rows(2)
-    relay_second("s2", student_slot)
     beats_first()
     pass_on(1)
     side_rows(1)
+    relay_second("s2", student_slot)
     far_rows(0)
-    student_pair()
+    beats_second()
     finish_all(hand)
     student = dot(place, r["incoming"][...].reshape(256, 512).astype(bf)).astype(bf)
     r["student"][...] = student
     shared["in"] = share_rows(0, student, 16, r["tin"], r["lin"])
     far_rows(1)
+    student_pair()
     send_sides(order[0])
-    beats_second()
-    finish_all(stage["s3"])
+    stage["s3"][0].wait()
     student = r["student"][...]
     pre_act = dot(student, full[0][...].reshape(512, 1536))
     shifted = pre_act - 4.0
-    soft = jnp.maximum(shifted, 0.0) + jnp.log1p(jnp.exp(-jnp.abs(shifted)))
+    decay = jnp.exp(-jnp.abs(shifted))
+    soft = jnp.maximum(shifted, 0.0) + jnp.log1p(decay)
     activated = (soft - 0.08 * pre_act - 0.035).astype(bf)
-    r["slope"][...] = jax.nn.sigmoid(shifted) - 0.08
-    features = (student.astype(f32) + dot(activated, full[1][...].reshape(1536, 512))).astype(bf)
+    r["slope"][...] = jnp.where(shifted >= 0.0, 1.0, decay) / (1.0 + decay) - 0.08
+    r["active"][...] = activated
+    relay_second("b2", beats_slots)
     send_sides(order[1])
+    stage["s3"][1].wait()
+    features = (student.astype(f32) + dot(r["active"][...], full[1][...].reshape(1536, 512))).astype(bf)
     shared["feat"] = share_rows(1, features, 16, r["tfeat"], r["lfeat"])
-    shared["act"] = share_rows(2, activated, 48, r["tact"], r["lact"])
-    relay_second("b2", beats_slots)
+    beats_share()
+    stage["s3"][2].wait()
     for k, width, start in TEACHERS:
         r["predicted"][:, start:start + width] = dot(features, full[2][:, :, :, :, start:start + width].reshape(512, width))
 
@@ -456,7 +460,7 @@
         phase2[n] = copies
 
     cp, _ = error_of(0)
-    beats_share()
+    shared["act"] = share_rows(2, r["active"][...], 48, r["tact"], r["lact"])
     finish_all([cp, shared["feat"]])
     start_group(0)
     beats_pair()
@@ -474,9 +478,9 @@
     act_grad = dot_t(feat_grad, full[1][...].reshape(1536, 512))
     rpre[0:128] = (act_grad * r["slope"][...]).astype(bf)
     cp = pair_send(7, rpre.at[pl.ds(0, 128)], rpre.at[pl.ds(128, 128)])
-    next_group(1)
     finish_all(late)
     start_group(2)
+    next_group(1)
     cp.wait()
     start_group(3)
 

time: 99.6 us -> 93.2 us (0.936)
  Pallas kernels: 98.1 us -> 91.7 us
    pallas_call x1, Pallas kernels: 96.2 us -> 89.8 us  [body(): pl.pallas_call(functools.partial(step_kernel, tuple(plan)), out_shape=jax...]
where the time goes in v8:
time: 93.2 us; the launch traced here: 93 us
  Pallas kernels  91.7 us (98%)
  between operations  1.29 us (1%)
    pallas_call x1, Pallas kernels, body(): pl.pallas_call(functools.partial(step_kernel, tuple(plan)), out_shape=jax...  89.8 us
    pallas_call x1, Pallas kernels, body(): pl.pallas_call(sum_kernel, out_shape=[jax.ShapeDtypeStruct((16, 1536), f3...  1.91 us

profile of v8, /device:TPU:0, one launch (start us, length us, event | category | flops | bytes accessed | tf_op | source)
XLA Modules:
  0.0 93.0 jit_solution(18407001156401095743)
XLA Ops:
  1.3 89.8 %shard_map.166.sums = bf16[4,16,6144]{2,1,0:T(8,128)(2,1)} custom-call(bf16[128,1280]{1,0:T(8,128)(2,1)} %refs_0_.1, bf16[128,768]{1,0:T(8,128)(2,1)} %refs_1_.1, bf16[128,1024]{1,0:T(8,128)(2,1)} %refs_2_.1, bf16[1280,1280]{1,0:T(8,128)(2,1)} %refs_3_.1, bf16[1280,1280]{1,0:T(8,128)(2,1)} %refs_4_.1, bf16[768,768]{1,0:T(8,128)(2,1)} %refs_5_.1, ...), custom_call_target="tpu_custom_call" | custom-call | tf_op jit(solution)/shard_map/pallas_call | solution.py:537
  91.1 1.9 %shard_map.167 = (f32[16,1536]{1,0:T(8,128)}, f32[48,512]{1,0:T(8,128)}, f32[16,3072]{1,0:T(8,128)}) custom-call(bf16[4,16,6144]{2,1,0:T(8,128)(2,1)} %shard_map.166.sums), custom_call_target="tpu_custom_call" | custom-call | tf_op jit(solution)/shard_map/pallas_call | solution.py:550

commit v9 on v8

--- a/solution.py
+++ b/solution.py
@@ -23,7 +23,7 @@
 MESH_ID = pl.DeviceIdType.MESH
 TEACHERS = ((2, WL, WH + WB), (0, WH, 0), (1, WB, WH))
 SPAN = 6144
-GROUP_COLUMNS = ((0, 1024), (1024, 1280), (2304, 2304), (4608, 1536))
+GROUP_COLUMNS = ((0, 1024), (1024, 1280), (2304, 768), (3072, 1536), (4608, 1536))
 
 
 def gelu(values):
@@ -74,7 +74,7 @@
         psem=dma((2,)), pys=dma((3,)), pyr=dma((3,)), gs=dma((96,)), gr=dma((96,)),
         hos=dma((32,)), hor=dma((32,)),
         xs=dma((8,)), xr=dma((8,)),
-        s1s=dma((4, 3)), s1r=dma((4, 3)), s2s=dma((4, 3)), s2r=dma((4, 3)), s3s=dma((4, 3)), s3r=dma((4, 3)),
+        s1s=dma((5, 3)), s1r=dma((5, 3)), s2s=dma((5, 3)), s2r=dma((5, 3)), s3s=dma((5, 3)), s3r=dma((5, 3)),
     )
     return plan
 
@@ -407,12 +407,11 @@
         return jnp.concatenate(tiles, axis=0)
 
     def products(n, a, store):
-        heads = block_rows(r["lfeat"], a) if n < 3 else None
-        if n < 2:
+        if n < 3:
+            heads = block_rows(r["lfeat"], a)
             _, width, start = TEACHERS[n]
             store(GROUP_COLUMNS[n][0], dot(heads, rerr[:, start:start + width]).reshape(4, 16, width))
-        elif n == 2:
-            store(2304, dot(heads, rerr[:, WH:WH + WB]).reshape(4, 16, WB))
+        elif n == 3:
             outs = dot(block_rows(r["lact"], a), rfg[...]).reshape(4, 48, 512)
             for m in range(3):
                 store(3072 + 512 * m, outs[:, 16 * m:16 * m + 16])
@@ -474,15 +473,17 @@
     cp, back = error_of(2)
     feat_grad = back.astype(bf)
     rfg[0:128] = feat_grad
-    late = [cp, pair_send(6, rfg.at[pl.ds(0, 128)], rfg.at[pl.ds(128, 128)])]
+    late = [pair_send(6, rfg.at[pl.ds(0, 128)], rfg.at[pl.ds(128, 128)])]
+    cp.wait()
+    start_group(2)
     act_grad = dot_t(feat_grad, full[1][...].reshape(1536, 512))
     rpre[0:128] = (act_grad * r["slope"][...]).astype(bf)
     cp = pair_send(7, rpre.at[pl.ds(0, 128)], rpre.at[pl.ds(128, 128)])
     finish_all(late)
-    start_group(2)
+    start_group(3)
     next_group(1)
     cp.wait()
-    start_group(3)
+    start_group(4)
 
     summed = {}
 
@@ -504,9 +505,12 @@
     next_group(3)
     finish_all(phase2[2])
     send_sums(2)
+    next_group(4)
     finish_all(phase2[3])
     send_sums(3)
-    for q in range(4):
+    finish_all(phase2[4])
+    send_sums(4)
+    for q in range(5):
         finish_all(summed[q])
 
 

time: 93.2 us -> 92.9 us (level)
  no operation moved by 1% of the time
where the time goes in v9:
time: 92.9 us; the launch traced here: 92.8 us
  Pallas kernels  91.5 us (98%)
  between operations  1.29 us (1%)
    pallas_call x1, Pallas kernels, body(): pl.pallas_call(functools.partial(step_kernel, tuple(plan)), out_shape=jax...  89.6 us
    pallas_call x1, Pallas kernels, body(): pl.pallas_call(sum_kernel, out_shape=[jax.ShapeDtypeStruct((16, 1536), f3...  1.91 us

profile of v9, /device:TPU:0, one launch (start us, length us, event | category | flops | bytes accessed | tf_op | source)
XLA Modules:
  0.0 92.8 jit_solution(379015433009108157)
XLA Ops:
  1.3 89.6 %shard_map.166.sums = bf16[4,16,6144]{2,1,0:T(8,128)(2,1)} custom-call(bf16[128,1280]{1,0:T(8,128)(2,1)} %refs_0_.1, bf16[128,768]{1,0:T(8,128)(2,1)} %refs_1_.1, bf16[128,1024]{1,0:T(8,128)(2,1)} %refs_2_.1, bf16[1280,1280]{1,0:T(8,128)(2,1)} %refs_3_.1, bf16[1280,1280]{1,0:T(8,128)(2,1)} %refs_4_.1, bf16[768,768]{1,0:T(8,128)(2,1)} %refs_5_.1, ...), custom_call_target="tpu_custom_call" | custom-call | tf_op jit(solution)/shard_map/pallas_call | solution.py:541
  90.8 1.9 %shard_map.167 = (f32[16,1536]{1,0:T(8,128)}, f32[48,512]{1,0:T(8,128)}, f32[16,3072]{1,0:T(8,128)}) custom-call(bf16[4,16,6144]{2,1,0:T(8,128)(2,1)} %shard_map.166.sums), custom_call_target="tpu_custom_call" | custom-call | tf_op jit(solution)/shard_map/pallas_call | solution.py:554

commit v10 on v9

--- a/solution.py
+++ b/solution.py
@@ -458,6 +458,18 @@
         r["own2"][:, cols] = total1(second)
         phase2[n] = copies
 
+    summed = {}
+
+    def send_sums(q):
+        start, width = GROUP_COLUMNS[q]
+        cols, ref_cols = slice(start, start + width), pl.ds(start, width)
+        total = r["own2"][:, cols]
+        for i in range(3):
+            total = total + r["recv2"][i, :, cols].astype(f32)
+        sums[y, :, cols] = total.astype(bf)
+        mine = sums.at[y, :, ref_cols]
+        summed[q] = [send(mine, mine, r["s3s"].at[q, d - 1], r["s3r"].at[q, d - 1], at_y(y + d)) for d in (2, 1, 3)]
+
     cp, _ = error_of(0)
     shared["act"] = share_rows(2, r["active"][...], 48, r["tact"], r["lact"])
     finish_all([cp, shared["feat"]])
@@ -479,29 +491,17 @@
     act_grad = dot_t(feat_grad, full[1][...].reshape(1536, 512))
     rpre[0:128] = (act_grad * r["slope"][...]).astype(bf)
     cp = pair_send(7, rpre.at[pl.ds(0, 128)], rpre.at[pl.ds(128, 128)])
+    finish_all(phase2[0])
+    send_sums(0)
     finish_all(late)
     start_group(3)
     next_group(1)
     cp.wait()
     start_group(4)
-
-    summed = {}
-
-    def send_sums(q):
-        start, width = GROUP_COLUMNS[q]
-        cols, ref_cols = slice(start, start + width), pl.ds(start, width)
-        total = r["own2"][:, cols]
-        for i in range(3):
-            total = total + r["recv2"][i, :, cols].astype(f32)
-        sums[y, :, cols] = total.astype(bf)
-        mine = sums.at[y, :, ref_cols]
-        summed[q] = [send(mine, mine, r["s3s"].at[q, d - 1], r["s3r"].at[q, d - 1], at_y(y + d)) for d in (2, 1, 3)]
-
-    finish_all(phase2[0])
-    send_sums(0)
+    next_group(2)
+
     finish_all(phase2[1])
     send_sums(1)
-    next_group(2)
     next_group(3)
     finish_all(phase2[2])
     send_sums(2)

time: 92.9 us -> 92.9 us (level)
  no operation moved by 1% of the time
where the time goes in v10:
time: 92.9 us; the launch traced here: 92.8 us
  Pallas kernels  91.5 us (98%)
  between operations  1.29 us (1%)
    pallas_call x1, Pallas kernels, body(): pl.pallas_call(functools.partial(step_kernel, tuple(plan)), out_shape=jax...  89.6 us
    pallas_call x1, Pallas kernels, body(): pl.pallas_call(sum_kernel, out_shape=[jax.ShapeDtypeStruct((16, 1536), f3...  1.91 us

profile of v10, /device:TPU:0, one launch (start us, length us, event | category | flops | bytes accessed | tf_op | source)
XLA Modules:
  0.0 92.8 jit_solution(15670629358781482726)
XLA Ops:
  1.3 89.6 %shard_map.166.sums = bf16[4,16,6144]{2,1,0:T(8,128)(2,1)} custom-call(bf16[128,1280]{1,0:T(8,128)(2,1)} %refs_0_.1, bf16[128,768]{1,0:T(8,128)(2,1)} %refs_1_.1, bf16[128,1024]{1,0:T(8,128)(2,1)} %refs_2_.1, bf16[1280,1280]{1,0:T(8,128)(2,1)} %refs_3_.1, bf16[1280,1280]{1,0:T(8,128)(2,1)} %refs_4_.1, bf16[768,768]{1,0:T(8,128)(2,1)} %refs_5_.1, ...), custom_call_target="tpu_custom_call" | custom-call | tf_op jit(solution)/shard_map/pallas_call | solution.py:541
  90.8 1.9 %shard_map.167 = (f32[16,1536]{1,0:T(8,128)}, f32[48,512]{1,0:T(8,128)}, f32[16,3072]{1,0:T(8,128)}) custom-call(bf16[4,16,6144]{2,1,0:T(8,128)(2,1)} %shard_map.166.sums), custom_call_target="tpu_custom_call" | custom-call | tf_op jit(solution)/shard_map/pallas_call | solution.py:554
